TPU v7x, 128 devices: a whole 4x4x4 slice. The times are simulated.
128 devices in a mesh: section: 4 (over x), dp: 32 (over y, z, core).
Axes of the slice: x: 4, y: 4, z: 4, core: 2. Of those that a mesh axis runs over, the one named last changes fastest.
Arguments:
- d_out: bfloat16 [4, 1536, 4096], P('section', 'dp'), may hold values from -6 to 6
- down_weight: bfloat16 [4, 11264, 4096], P('section', 'dp'), may hold values from -0.0546875 to 0.0546875
- gate_weight: bfloat16 [4, 11264, 4096], P('section', 'dp'), may hold values from -0.0546875 to 0.0546875
- up_weight: bfloat16 [4, 11264, 4096], P('section', 'dp'), may hold values from -0.0546875 to 0.0546875
- gate_pre: bfloat16 [4, 1536, 11264], P('section', 'dp'), may hold values from -6 to 6
- up_val: bfloat16 [4, 1536, 11264], P('section', 'dp'), may hold values from -6 to 6
- block_rows: int32 [4, 64], P('section'), may hold values from 0 to 87, as said below
- block_cols: int32 [4, 64], P('section'), may hold values from 0 to 31, as said below
- block_owner: int32 [4, 64], P('section'), may hold values from 0 to 31, as said below
Outputs:
- grad_input: bfloat16 [4, 1536, 4096], P('section', 'dp')
- block_grads: bfloat16 [4, 96, 128, 128], P('section', 'dp')
Inputs may be any that keep to these rules, and one draw needn't show every extreme that they name: `block_rows`: the 64 (row, column) pairs of a section are all different. `block_cols`: the 64 (row, column) pairs of a section are all different. `block_owner`: in each section no replica owns more than 3 blocks, and one owns exactly 3.
All inputs are finite; a program needn't handle non-finite values.
Results may differ from a plain program's by a relative error of at most 0.018.
Values may be sent and summed in bfloat16 or wider, within the bound.
A program may use at most 128 MiB of HBM per device.

v0:
```python
import jax
import jax.numpy as jnp
from jax import lax
from jax.sharding import PartitionSpec as P

CAP = 3


def passed_along(value, axis, by):
    devices = lax.axis_size(axis)
    pairs = [(i, i + by) for i in range(devices) if 0 <= i + by < devices]
    return lax.ppermute(value, axis, pairs)


def in_blocks(value, dim, devices):
    before, after = (value.shape[:dim], value.shape[dim + 1 :])
    return jnp.moveaxis(value.reshape(*before, devices, -1, *after), dim, 0)


def sum_at_owner(value, axis, dim):
    devices = lax.axis_size(axis)
    blocks = lax.all_to_all(in_blocks(value, dim, devices), axis, 0, 0, tiled=True)
    return jnp.sum(blocks.astype(jnp.float32), axis=0)


def laid_out(blocks, dim):
    blocks = jnp.moveaxis(blocks, 0, dim)
    dims = blocks.shape
    return blocks.reshape(*dims[:dim], dims[dim] * dims[dim + 1], *dims[dim + 2 :])


def from_everyone(value, axis):
    devices = lax.axis_size(axis)
    return lax.all_to_all(
        jnp.broadcast_to(value[None], (devices, *value.shape)), axis, 0, 0, tiled=True
    )


def gather_directly(value, axis, dim):
    return laid_out(from_everyone(value, axis), dim)


def gelu_pair(values):
    coeff = 0.7978845608
    cubic = values * values * values
    tangent = jnp.tanh(coeff * (values + 0.044715 * cubic))
    activated = 0.5 * values * (1.0 + tangent)
    slope = 0.5 * (1.0 + tangent) + 0.5 * values * (1.0 - tangent * tangent) * coeff * (
        1.0 + 3.0 * 0.044715 * values * values
    )
    return (activated, slope)


def owner_slots(owners):
    count_blocks = owners.shape[0]
    same = owners[:, None] == owners[None, :]
    index_list = jnp.arange(count_blocks, dtype=jnp.int32)
    earlier = index_list[None, :] < index_list[:, None]
    return jnp.sum((same & earlier).astype(jnp.int32), axis=1)


def shards(
    d_out,
    down_weight,
    gate_weight,
    up_weight,
    gate_pre,
    up_val,
    block_rows,
    block_cols,
    block_owner,
):
    grad_rows = d_out[0]
    w_shard = down_weight[0]
    w_gate = gate_weight[0]
    w_up = up_weight[0]
    replicas = lax.axis_size("dp")
    tok_rows = grad_rows.shape[0]
    model_width = grad_rows.shape[1]
    hidden_width = gate_pre.shape[2]
    columns = lax.dot_general(
        lax.all_gather(grad_rows, "dp", axis=0, tiled=True),
        w_shard,
        (((1,), (1,)), ((), ())),
        preferred_element_type=jnp.float32,
    ).astype(jnp.bfloat16)
    returned = lax.all_to_all(columns, "dp", split_axis=0, concat_axis=1, tiled=True)
    gate_val = gate_pre[0].astype(jnp.float32)
    up_vals = up_val[0].astype(jnp.float32)
    activated, slope = gelu_pair(gate_val)
    dh_wide = returned.astype(jnp.float32)
    local_gate = (dh_wide * up_vals * slope).astype(jnp.bfloat16)
    local_up = (dh_wide * activated).astype(jnp.bfloat16)
    gate_units, up_units = (
        lax.all_to_all(local_gate, "dp", split_axis=1, concat_axis=0, tiled=True),
        lax.all_to_all(local_up, "dp", split_axis=1, concat_axis=0, tiled=True),
    )
    summed_input = lax.psum_scatter(
        (
            jnp.dot(gate_units, w_gate, preferred_element_type=jnp.float32)
            + jnp.dot(up_units, w_up, preferred_element_type=jnp.float32)
        ).astype(jnp.bfloat16),
        "dp",
        scatter_dimension=0,
        tiled=True,
    )
    grad_input = passed_along(summed_input, "section", -1)
    hidden = (activated * up_vals).astype(jnp.bfloat16)
    row_ids = block_rows[0]
    col_ids = block_cols[0]
    owners = block_owner[0]
    count_blocks = row_ids.shape[0]
    hidden_sel = jnp.take(hidden.reshape(tok_rows, hidden_width // 128, 128), row_ids, axis=1)
    grad_sel = jnp.take(grad_rows.reshape(tok_rows, model_width // 128, 128), col_ids, axis=1)
    partial_value = jnp.einsum(
        "tnf,tnd->nfd", hidden_sel, grad_sel, preferred_element_type=jnp.float32
    )
    partial_value = lax.optimization_barrier(partial_value.astype(jnp.bfloat16)).astype(jnp.float32)
    slots = owner_slots(owners)
    scale = 1.0 / replicas
    share = sum_at_owner(partial_value.astype(jnp.bfloat16), "dp", 0)
    rounded = (share * scale).astype(jnp.bfloat16)
    every_block = gather_directly(rounded, "dp", 0)
    owner_index = lax.axis_index("dp")
    slot_list = jnp.arange(CAP, dtype=jnp.int32)
    picked = (owners[None, :] == owner_index) & (slots[None, :] == slot_list[:, None])
    block_list = jnp.arange(count_blocks, dtype=jnp.int32)
    chosen = jnp.sum(jnp.where(picked, block_list[None, :], 0), axis=1)
    present = jnp.any(picked, axis=1)
    result = jnp.where(
        present[:, None, None], jnp.take(every_block, chosen, axis=0), jnp.zeros((), jnp.bfloat16)
    )
    return (grad_input[None], result[None])


def solution(mesh):
    return jax.shard_map(
        shards,
        mesh=mesh,
        in_specs=(
            P("section", "dp", None),
            P("section", "dp", None),
            P("section", "dp", None),
            P("section", "dp", None),
            P("section", "dp", None),
            P("section", "dp", None),
            P("section", None),
            P("section", None),
            P("section", None),
        ),
        out_specs=(P("section", "dp", None), P("section", "dp", None, None)),
        check_vma=False,
    )
```

profile of v0, /device:TPU:0, one launch (start us, length us, event | category | flops | bytes accessed | tf_op | source)
XLA Modules:
  0.0 323.6 jit_solution(16928282081733721958)
XLA Ops:
  7.9 67.8 %all-gather.3.cloned.1.call-done = bf16[1,1536,4096]{2,1,0:T(8,128)(2,1)} async-done(((bf16[1,48,4096]{2,1,0:T(8,128)(2,1)}), bf16[1,1536,4096]{2,1,0:T(8,128)(2,1)}) %all-gather.3.cloned.1.call-update) | async-done | bytes 12582928 | tf_op jit(solution)/shard_map/all_gather | solution.py:82
  75.7 11.1 %fusion.6 = bf16[1536,352]{0,1:T(8,128)(2,1)} fusion(bf16[1,352,4096]{2,1,0:T(8,128)(2,1)} %param.10, bf16[1,1536,4096]{2,1,0:T(8,128)(2,1)} %all-gather.3.cloned.1.call-done), kind=kOutput, calls=%fused_computation.14 | convolution fusion | flops 4429725696 | bytes 16547840 | tf_op jit(solution)/shard_map/dot_general | solution.py:81
  86.8 2.4 copy.36
  89.2 5.6 %all-to-all-start = ((bf16[32,48,352]{2,1,0:T(8,128)(2,1)}), bf16[32,48,352]{2,1,0:T(8,128)(2,1)}, u32[]{:S(2)}, u32[]{:S(2)}) async-start(bf16[32,48,352]{2,1,0:T(8,128)(2,1)} %bitcast.79), calls=%async_computation | async-start | bytes 2359296 | tf_op jit(solution)/shard_map/all_to_all | solution.py:87
  94.8 3.8 %reshape.139 = f32[48,32,352]{2,1,0:T(8,128)} reshape(bf16[1,48,11264]{2,1,0:T(8,128)(2,1)} %param.13) | data formatting | bytes 3244032 | tf_op jit(solution)/shard_map/convert_element_type | solution.py:88
  98.6 3.8 %reshape.138 = f32[48,32,352]{2,1,0:T(8,128)} reshape(bf16[1,48,11264]{2,1,0:T(8,128)(2,1)} %param.14) | data formatting | bytes 3244032 | tf_op jit(solution)/shard_map/convert_element_type | solution.py:89
  102.4 10.6 %all-to-all-done = bf16[32,48,352]{2,1,0:T(8,128)(2,1)} async-done(((bf16[32,48,352]{2,1,0:T(8,128)(2,1)}), bf16[32,48,352]{2,1,0:T(8,128)(2,1)}, u32[]{:S(2)}, u32[]{:S(2)}) %all-to-all-start) | async-done | bytes 1081376 | tf_op jit(solution)/shard_map/all_to_all | solution.py:87
  113.0 5.4 %fusion.20 = (bf16[48,32,352]{2,0,1:T(8,128)(2,1)}, bf16[48,32,352]{2,0,1:T(8,128)(2,1)S(1)}) fusion(bf16[32,48,352]{2,1,0:T(8,128)(2,1)} %all-to-all-done, f32[48,32,352]{2,1,0:T(8,128)} %reshape.139, f32[48,32,352]{2,1,0:T(8,128)} %reshape.138), kind=kLoop, calls=%fused_computation.26 | loop fusion | flops 12976128 | bytes 7569408 | tf_op jit(solution)/shard_map/convert_element_type | solution.py:93
  118.4 23.0 %all_to_all.55 = bf16[48,32,352]{2,0,1:T(8,128)(2,1)} all-to-all(bf16[48,32,352]{2,0,1:T(8,128)(2,1)S(1)} %get-tuple-element.3), channel_id=1, replica_groups=mesh['section'=4,'dp'=32] {'dp'}, dimensions={1} | all-to-all | bytes 2162688 | tf_op jit(solution)/shard_map/all_to_all | solution.py:95
  141.4 4.7 %all-to-all-start.2 = ((bf16[48,32,352]{2,0,1:T(8,128)(2,1)}), bf16[48,32,352]{2,0,1:T(8,128)(2,1)}, u32[]{:S(2)}, u32[]{:S(2)}) async-start(bf16[48,32,352]{2,0,1:T(8,128)(2,1)} %get-tuple-element.2), calls=%async_computation.2 | async-start | bytes 2359296 | tf_op jit(solution)/shard_map/all_to_all | solution.py:96
  146.3 13.0 %fusion.3 = f32[1536,4096]{1,0:T(8,128)} fusion(bf16[1536,352]{1,0:T(8,128)(2,1)} %bitcast.78, bf16[1,352,4096]{2,1,0:T(8,128)(2,1)S(1)} %copy-done), kind=kOutput, calls=%fused_computation.11 | convolution fusion | flops 4429185024 | bytes 29130752 | tf_op jit(solution)/shard_map/dot_general | solution.py:100
  159.3 5.0 %all-to-all-done.2 = bf16[48,32,352]{2,0,1:T(8,128)(2,1)} async-done(((bf16[48,32,352]{2,0,1:T(8,128)(2,1)}), bf16[48,32,352]{2,0,1:T(8,128)(2,1)}, u32[]{:S(2)}, u32[]{:S(2)}) %all-to-all-start.2) | async-done | bytes 1081376 | tf_op jit(solution)/shard_map/all_to_all | solution.py:96
  164.3 15.6 %add_convert_fusion = bf16[1536,4096]{1,0:T(8,128)(2,1)} fusion(f32[1536,4096]{1,0:T(8,128)} %fusion.3, bf16[1536,352]{1,0:T(8,128)(2,1)} %bitcast.8, bf16[1,352,4096]{2,1,0:T(8,128)(2,1)} %param.12), kind=kOutput, calls=%fused_computation.3 | convolution fusion | flops 4441767936 | bytes 41713664 | tf_op jit(solution)/shard_map/dot_general | solution.py:101
  182.8 1.7 copy.52
  184.5 1.5 gather_fusion.1
  186.1 3.6 %fusion.28 = bf16[48,88,128]{2,0,1:T(8,128)(2,1)} fusion(f32[48,88,128]{2,1,0:T(8,128)S(1)} %bitcast.75, f32[48,88,128]{2,1,0:T(8,128)} %bitcast.76), kind=kLoop, calls=%fused_computation.34 | loop fusion | flops 5406720 | bytes 5406720 | tf_op jit(solution)/shard_map/convert_element_type | solution.py:108
  189.7 2.0 gather_fusion
  191.8 2.2 convolution_convert_fusion
  193.9 31.8 %all_to_all.56 = bf16[32,2,128,128]{3,2,1,0:T(8,128)(2,1)S(1)} all-to-all(bf16[32,2,128,128]{3,2,1,0:T(8,128)(2,1)S(1)} %bitcast.77), channel_id=1, replica_groups=mesh['section'=4,'dp'=32] {'dp'}, dimensions={0} | all-to-all | bytes 4194304 | tf_op jit(solution)/shard_map/all_to_all | solution.py:22
  226.1 1.8 broadcast_in_dim.76
  227.9 4.9 %all-to-all-start.4 = ((bf16[32,2,128,128]{3,2,1,0:T(8,128)(2,1)}), bf16[32,2,128,128]{3,2,1,0:T(8,128)(2,1)}, u32[]{:S(2)}, u32[]{:S(2)}) async-start(bf16[32,2,128,128]{3,2,1,0:T(8,128)(2,1)} %broadcast_in_dim.76), calls=%async_computation.5 | async-start | bytes 4194304 | tf_op jit(solution)/shard_map/all_to_all | solution.py:34
  233.2 71.7 %reduce-scatter.2.cloned.1.call-done = bf16[48,4096]{1,0:T(8,128)(2,1)} async-done(((bf16[1536,4096]{1,0:T(8,128)(2,1)}), bf16[48,4096]{1,0:T(8,128)(2,1)}) %reduce-scatter.2.cloned.1.call-update) | async-done | bytes 393232 | tf_op jit(solution)/shard_map/reduce_scatter | solution.py:98
  306.3 2.2 gather_fusion.2
  309.2 6.9 %collective-permute-done = bf16[48,4096]{1,0:T(8,128)(2,1)S(1)} collective-permute-done((bf16[48,4096]{1,0:T(8,128)(2,1)}, bf16[48,4096]{1,0:T(8,128)(2,1)S(1)}, u32[]{:S(2)}, u32[]{:S(2)}) %collective-permute-start) | collective-permute-done | bytes 393248 | tf_op jit(solution)/shard_map/ppermute | solution.py:12
  (43 shorter events, 7.4 us)
Async XLA Ops:
  7.2 139.1 %copy-start = (bf16[1,352,4096]{2,1,0:T(8,128)(2,1)S(1)}, bf16[1,352,4096]{2,1,0:T(8,128)(2,1)}, u32[]{:S(2)}) copy-start(bf16[1,352,4096]{2,1,0:T(8,128)(2,1)} %param.11) | copy-start | bytes 8650756
  7.2 68.5 %all-gather.3.cloned.1.call-start = ((), (), s32[]{:S(2)}) async-start(), calls=%async_computation.7 | async-start | bytes 12976128 | tf_op jit(solution)/shard_map/all_gather | solution.py:82
  89.2 23.8 %all-to-all-start = ((bf16[32,48,352]{2,1,0:T(8,128)(2,1)}), bf16[32,48,352]{2,1,0:T(8,128)(2,1)}, u32[]{:S(2)}, u32[]{:S(2)}) async-start(bf16[32,48,352]{2,1,0:T(8,128)(2,1)} %bitcast.79), calls=%async_computation | async-start | bytes 2359296 | tf_op jit(solution)/shard_map/all_to_all | solution.py:87
  141.4 22.9 %all-to-all-start.2 = ((bf16[48,32,352]{2,0,1:T(8,128)(2,1)}), bf16[48,32,352]{2,0,1:T(8,128)(2,1)}, u32[]{:S(2)}, u32[]{:S(2)}) async-start(bf16[48,32,352]{2,0,1:T(8,128)(2,1)} %get-tuple-element.2), calls=%async_computation.2 | async-start | bytes 2359296 | tf_op jit(solution)/shard_map/all_to_all | solution.py:96
  146.1 158.8 %reduce-scatter.2.cloned.1.call-start = ((), (), s32[]{:S(2)}) async-start(), calls=%async_computation.6 | async-start | bytes 12976128 | tf_op jit(solution)/shard_map/reduce_scatter | solution.py:98
  179.9 1.0 copy-start.4
  179.9 1.4 copy-start.2
  181.4 1.2 copy-start.3
  182.8 1.8 copy-start.5
  182.8 3.3 %copy-start.6 = (s32[1,64]{1,0:T(1,128)S(1)}, s32[1,64]{1,0:T(1,128)}, u32[]{:S(2)}) copy-start(s32[1,64]{1,0:T(1,128)} %param.15) | copy-start | bytes 772
  226.0 90.8 %copy-start.1 = (bf16[1,352,4096]{2,1,0:T(8,128)(2,1)S(1)}, bf16[1,352,4096]{2,1,0:T(8,128)(2,1)}, u32[]{:S(2)}) copy-start(bf16[1,352,4096]{2,1,0:T(8,128)(2,1)} %param.11) | copy-start | bytes 8650756
  227.9 5.0 %copy-start.7 = (s32[1,64]{1,0:T(1,128)S(1)}, s32[1,64]{1,0:T(1,128)}, u32[]{:S(2)}) copy-start(s32[1,64]{1,0:T(1,128)} %param.17) | copy-start | bytes 772
  227.9 78.4 %all-to-all-start.4 = ((bf16[32,2,128,128]{3,2,1,0:T(8,128)(2,1)}), bf16[32,2,128,128]{3,2,1,0:T(8,128)(2,1)}, u32[]{:S(2)}, u32[]{:S(2)}) async-start(bf16[32,2,128,128]{3,2,1,0:T(8,128)(2,1)} %broadcast_in_dim.76), calls=%async_computation.5 | async-start | bytes 4194304 | tf_op jit(solution)/shard_map/all_to_all | solution.py:34
  304.8 11.2 %collective-permute-start = (bf16[48,4096]{1,0:T(8,128)(2,1)}, bf16[48,4096]{1,0:T(8,128)(2,1)S(1)}, u32[]{:S(2)}, u32[]{:S(2)}) collective-permute-start(bf16[48,4096]{1,0:T(8,128)(2,1)} %reduce-scatter.2.cloned.1.call-done), channel_id=1, source_target_pairs={{32,0},{64,32},{96,64},{33,1},{65,33},{97,65},{34,2},{66,34},{98,6... | collective-permute-start | bytes 1179656 | tf_op jit(solution)/shard_map/ppermute | solution.py:12
Sparse Core Ops, SparseCore 0:
  10.2 65.4 all-gather.2
  180.0 124.7 reduce-scatter.1
where the time goes:
time: 324 us
  waiting for transfers between devices  163 us (50%)
  blocking collectives  54.7 us (17%)
  matrix products  41.9 us (13%)
  local copies, waits for them, and re-layouts  22.6 us (7%)
  starting transfers between devices  16.7 us (5%)
  between operations  14.2 us (4%)
  other arithmetic  10.8 us (3%)
    reduce_scatter x1, waiting for transfers between devices, shards(): lax.psum_scatter((jnp.dot(gate_units, w_gate, preferred_element_type=jnp....  71.7 us
    all_gather x1, waiting for transfers between devices, shards(): lax.all_gather(grad_rows, 'dp', axis=0, tiled=True)  67.8 us
    all_to_all x1, blocking collectives, sum_at_owner(): lax.all_to_all(in_blocks(value, dim, devices), axis, 0, 0, tiled=True)  31.8 us
    all_to_all x1, blocking collectives, shards(): lax.all_to_all(local_gate, 'dp', split_axis=1, concat_axis=0, tiled=True)  23 us
    dot_general x1, matrix products, shards(): jnp.dot(up_units, w_up, preferred_element_type=jnp.float32)  15.6 us
    dot_general x1, matrix products, shards(): jnp.dot(gate_units, w_gate, preferred_element_type=jnp.float32)  13 us
    dot_general x1, matrix products, shards(): lax.dot_general(lax.all_gather(grad_rows, 'dp', axis=0, tiled=True), w_sh...  11.1 us
    all_to_all x1, waiting for transfers between devices, shards(): lax.all_to_all(columns, 'dp', split_axis=0, concat_axis=1, tiled=True)  10.6 us
  transfers between devices with their start and end apart: 6, of which 5 were waited for; matrix products, arithmetic and copies ran while one was open for 12% of the time, Pallas kernels for 0%

commit v1 on v0

v1 whole, which is shorter than its diff:
```python
import jax
import jax.numpy as jnp
from jax import lax
from jax.sharding import PartitionSpec as P

CAP = 3


def passed_along(value, axis, by):
    devices = lax.axis_size(axis)
    pairs = [(i, i + by) for i in range(devices) if 0 <= i + by < devices]
    return lax.ppermute(value, axis, pairs)


def gelu_pair(values):
    coeff = 0.7978845608
    cubic = values * values * values
    tangent = jnp.tanh(coeff * (values + 0.044715 * cubic))
    activated = 0.5 * values * (1.0 + tangent)
    slope = 0.5 * (1.0 + tangent) + 0.5 * values * (1.0 - tangent * tangent) * coeff * (
        1.0 + 3.0 * 0.044715 * values * values
    )
    return (activated, slope)


def owner_slots(owners):
    count_blocks = owners.shape[0]
    same = owners[:, None] == owners[None, :]
    index_list = jnp.arange(count_blocks, dtype=jnp.int32)
    earlier = index_list[None, :] < index_list[:, None]
    return jnp.sum((same & earlier).astype(jnp.int32), axis=1)


def shards(
    d_out,
    down_weight,
    gate_weight,
    up_weight,
    gate_pre,
    up_val,
    block_rows,
    block_cols,
    block_owner,
):
    grad_rows = d_out[0]
    w_shard = down_weight[0]
    w_gate = gate_weight[0]
    w_up = up_weight[0]
    tok_rows = grad_rows.shape[0]
    replicas = lax.axis_size("dp")
    row_ids = block_rows[0]
    col_ids = block_cols[0]
    owners = block_owner[0]
    count_blocks = row_ids.shape[0]
    position = owners * CAP + owner_slots(owners)
    slot_ids = jnp.arange(replicas * CAP, dtype=jnp.int32)
    match = position[None, :] == slot_ids[:, None]
    block_list = jnp.arange(count_blocks, dtype=jnp.int32)
    slot_rows = jnp.sum(jnp.where(match, row_ids[None, :], 0), axis=1)
    owner_index = lax.axis_index("dp")
    my_slots = owner_index * CAP + jnp.arange(CAP, dtype=jnp.int32)
    my_match = position[None, :] == my_slots[:, None]
    my_cols = jnp.sum(jnp.where(my_match, col_ids[None, :], 0), axis=1)
    present = jnp.any(my_match, axis=1)

    gate_local, up_local = gate_pre[0], up_val[0]
    gate_units = lax.all_to_all(gate_local, "dp", split_axis=1, concat_axis=0, tiled=True)
    up_units = lax.all_to_all(up_local, "dp", split_axis=1, concat_axis=0, tiled=True)
    every_row = lax.all_gather(grad_rows, "dp", axis=0, tiled=True)

    def in_slots(value):
        blocks = value.reshape(tok_rows, -1, 128)
        return jnp.take(blocks, slot_rows, axis=1).astype(jnp.float32)

    sel_gate, sel_up = in_slots(gate_local), in_slots(up_local)
    hidden_sel = (gelu_pair(sel_gate)[0] * sel_up).astype(jnp.bfloat16)
    hidden_mine = lax.all_to_all(hidden_sel, "dp", split_axis=1, concat_axis=0, tiled=True)

    dhidden = lax.dot_general(
        every_row, w_shard, (((1,), (1,)), ((), ())), preferred_element_type=jnp.float32
    ).astype(jnp.bfloat16)
    activated, slope = gelu_pair(gate_units.astype(jnp.float32))
    dh_wide = dhidden.astype(jnp.float32)
    local_gate = (dh_wide * up_units.astype(jnp.float32) * slope).astype(jnp.bfloat16)
    local_up = (dh_wide * activated).astype(jnp.bfloat16)
    summed_input = lax.psum_scatter(
        (
            jnp.dot(local_gate, w_gate, preferred_element_type=jnp.float32)
            + jnp.dot(local_up, w_up, preferred_element_type=jnp.float32)
        ).astype(jnp.bfloat16),
        "dp",
        scatter_dimension=0,
        tiled=True,
    )
    grad_input = passed_along(summed_input, "section", -1)
    grad_sel = jnp.take(every_row.reshape(every_row.shape[0], -1, 128), my_cols, axis=1)
    mine = jnp.einsum("tnf,tnd->nfd", hidden_mine, grad_sel, preferred_element_type=jnp.float32)
    mine = (mine * (1.0 / replicas)).astype(jnp.bfloat16)
    result = jnp.where(present[:, None, None], mine, jnp.zeros((), jnp.bfloat16))
    return (grad_input[None], result[None])


def solution(mesh):
    return jax.shard_map(
        shards,
        mesh=mesh,
        in_specs=(
            P("section", "dp", None),
            P("section", "dp", None),
            P("section", "dp", None),
            P("section", "dp", None),
            P("section", "dp", None),
            P("section", "dp", None),
            P("section", None),
            P("section", None),
            P("section", None),
        ),
        out_specs=(P("section", "dp", None), P("section", "dp", None, None)),
        check_vma=False,
    )
```

time: 324 us -> 294 us (0.907)
  blocking collectives: 54.7 us -> 0 us
  local copies, waits for them, and re-layouts: 22.6 us -> 68.6 us
  waiting for transfers between devices: 163 us -> 137 us
  starting transfers between devices: 16.7 us -> 20 us
    all_gather x1, waiting for transfers between devices: 67.8 us -> 9.22 us  [shards(): every_row = lax.all_gather(grad_rows, 'dp', axis=0, tiled=True)]
    all_to_all x2 -> x0, blocking collectives: 54.7 us -> none  [the longest x1 31.8 us: sum_at_owner(): lax.all_to_all(in_blocks(value, dim, devices), axis, 0, 0, tiled=True)]
    all_to_all x3, waiting for transfers between devices: 15.6 us -> 39.7 us  [the longest x1 21.9 us: shards(): lax.all_to_all(up_local, 'dp', split_axis=1, concat_axis=0, tiled=True)]
    all_gather x0 -> x1, local copies, waits for them, and re-layouts: none -> 16.6 us  [shards(): every_row = lax.all_gather(grad_rows, 'dp', axis=0, tiled=True)]
    reshape x0 -> x1, local copies, waits for them, and re-layouts: none -> 16.2 us  [shards(): every_row.reshape(every_row.shape[0], -1, 128)]
    reduce_scatter x1, waiting for transfers between devices: 71.7 us -> 87.4 us  [shards(): lax.psum_scatter((jnp.dot(local_gate, w_gate, preferred_element_type=jnp....]
    all_to_all x0 -> x5, local copies, waits for them, and re-layouts: none -> 13.9 us  [the longest x2 6.46 us: shards(): lax.all_to_all(gate_local, 'dp', split_axis=1, concat_axis=0, tiled=True)]
    ppermute x1, waiting for transfers between devices: 6.9 us -> 0.01 us  [passed_along(): return lax.ppermute(value, axis, pairs)]
  transfers between devices with their start and end apart: 6 -> 6, of which waited for: 5 -> 4; matrix products, arithmetic and copies ran while one was open for 12% -> 24% of each run, Pallas kernels for 0% -> 0%
where the time goes in v1:
time: 294 us; the launch traced here: 291 us
  waiting for transfers between devices  137 us (47%)
  local copies, waits for them, and re-layouts  68.6 us (23%)
  matrix products  40.4 us (14%)
  starting transfers between devices  20 us (7%)
  between operations  14.2 us (5%)
  other arithmetic  10.6 us (4%)
    reduce_scatter x1, waiting for transfers between devices, shards(): lax.psum_scatter((jnp.dot(local_gate, w_gate, preferred_element_type=jnp....  87.4 us
    all_to_all x1, waiting for transfers between devices, shards(): lax.all_to_all(up_local, 'dp', split_axis=1, concat_axis=0, tiled=True)  21.9 us
    all_to_all x1, waiting for transfers between devices, shards(): lax.all_to_all(gate_local, 'dp', split_axis=1, concat_axis=0, tiled=True)  17.8 us
    all_gather x1, local copies, waits for them, and re-layouts, shards(): every_row = lax.all_gather(grad_rows, 'dp', axis=0, tiled=True)  16.6 us
    dot_general x1, matrix products, shards(): jnp.dot(local_up, w_up, preferred_element_type=jnp.float32)  16.5 us
    reshape x1, local copies, waits for them, and re-layouts, shards(): every_row.reshape(every_row.shape[0], -1, 128)  16.2 us
    dot_general x1, matrix products, shards(): jnp.dot(local_gate, w_gate, preferred_element_type=jnp.float32)  12.3 us
    all_gather x1, waiting for transfers between devices, shards(): every_row = lax.all_gather(grad_rows, 'dp', axis=0, tiled=True)  9.22 us
  transfers between devices with their start and end apart: 6, of which 4 were waited for; matrix products, arithmetic and copies ran while one was open for 24% of the time, Pallas kernels for 0%

profile of v1, /device:TPU:0, one launch (start us, length us, event | category | flops | bytes accessed | tf_op | source)
XLA Modules:
  0.0 290.7 jit_solution(3640510001825329475)
XLA Ops:
  7.9 3.8 %all_to_all.35 = bf16[48,32,352]{2,1,0:T(8,128)(2,1)} reshape(bf16[1,48,11264]{2,1,0:T(8,128)(2,1)} %param.15) | data formatting | bytes 2162688 | tf_op jit(solution)/shard_map/all_to_all | solution.py:67
  11.7 2.7 copy.59
  14.4 8.6 %all-to-all-start.1 = ((bf16[48,32,352]{2,0,1:T(8,128)(2,1)}), bf16[48,32,352]{2,0,1:T(8,128)(2,1)}, u32[]{:S(2)}, u32[]{:S(2)}) async-start(bf16[48,32,352]{2,0,1:T(8,128)(2,1)} %copy.59), calls=%async_computation.1 | async-start | bytes 2359296 | tf_op jit(solution)/shard_map/all_to_all | solution.py:67
  22.9 3.7 %all_to_all.33 = bf16[48,32,352]{2,1,0:T(8,128)(2,1)} reshape(bf16[1,48,11264]{2,1,0:T(8,128)(2,1)} %param.16) | data formatting | bytes 2162688 | tf_op jit(solution)/shard_map/all_to_all | solution.py:68
  26.6 2.7 copy.57
  29.3 17.8 %all-to-all-done.1 = bf16[48,32,352]{2,0,1:T(8,128)(2,1)} async-done(((bf16[48,32,352]{2,0,1:T(8,128)(2,1)}), bf16[48,32,352]{2,0,1:T(8,128)(2,1)}, u32[]{:S(2)}, u32[]{:S(2)}) %all-to-all-start.1) | async-done | bytes 1081376 | tf_op jit(solution)/shard_map/all_to_all | solution.py:67
  47.1 4.7 %all-to-all-start = ((bf16[48,32,352]{2,0,1:T(8,128)(2,1)}), bf16[48,32,352]{2,0,1:T(8,128)(2,1)}, u32[]{:S(2)}, u32[]{:S(2)}) async-start(bf16[48,32,352]{2,0,1:T(8,128)(2,1)} %copy.57), calls=%async_computation | async-start | bytes 2359296 | tf_op jit(solution)/shard_map/all_to_all | solution.py:68
  52.0 3.0 %convert_element_type.67 = f32[48,32,352]{2,0,1:T(8,128)} convert(bf16[48,32,352]{2,0,1:T(8,128)(2,1)} %all-to-all-done.1) | non-fusion elementwise | flops 540672 | bytes 3244032 | tf_op jit(solution)/shard_map/convert_element_type | solution.py:82
  55.0 3.4 %copy.63 = f32[1536,352]{0,1:T(8,128)} copy(f32[1536,352]{1,0:T(8,128)} %bitcast.70) | data formatting | bytes 4325376 | tf_op jit(solution)/shard_map/convert_element_type | solution.py:82
  58.3 21.9 %all-to-all-done = bf16[48,32,352]{2,0,1:T(8,128)(2,1)} async-done(((bf16[48,32,352]{2,0,1:T(8,128)(2,1)}), bf16[48,32,352]{2,0,1:T(8,128)(2,1)}, u32[]{:S(2)}, u32[]{:S(2)}) %all-to-all-start) | async-done | bytes 1081376 | tf_op jit(solution)/shard_map/all_to_all | solution.py:68
  80.3 2.8 convert_element_type.66
  83.1 3.2 %copy.58 = f32[1536,352]{0,1:T(8,128)} copy(f32[1536,352]{1,0:T(8,128)} %bitcast.71) | data formatting | bytes 4325376 | tf_op jit(solution)/shard_map/convert_element_type | solution.py:84
  86.4 9.2 %all-gather.3.cloned.1.call-done = bf16[1,1536,4096]{2,1,0:T(8,128)(2,1)} async-done(((bf16[1,48,4096]{2,1,0:T(8,128)(2,1)}), bf16[1,1536,4096]{2,1,0:T(8,128)(2,1)}) %all-gather.3.cloned.1.call-update) | async-done | bytes 12582928 | tf_op jit(solution)/shard_map/all_gather | solution.py:69
  95.6 8.7 %fusion.11 = f32[1536,352]{0,1:T(8,128)S(1)} fusion(bf16[1,352,4096]{2,1,0:T(8,128)(2,1)} %param.12, bf16[1,1536,4096]{2,1,0:T(8,128)(2,1)} %all-gather.3.cloned.1.call-done), kind=kOutput, calls=%fused_computation.17 | convolution fusion | flops 4430266368 | bytes 17629184 | tf_op jit(solution)/shard_map/dot_general | solution.py:79
  105.7 12.3 %fusion.3 = f32[1536,4096]{1,0:T(8,128)} fusion(bf16[1,352,4096]{2,1,0:T(8,128)(2,1)S(1)} %copy-done, f32[1536,352]{0,1:T(8,128)S(1)} %copy-done.2, f32[1536,352]{0,1:T(8,128)S(1)} %fusion.11, f32[1536,352]{0,1:T(8,128)S(1)} %copy-done.4), kind=kOutput, calls=%fused_computation.13 | convolution fusion | flops 4439998464 | bytes 34537472 | tf_op jit(solution)/shard_map/dot_general | solution.py:88
  118.0 16.5 %add_convert_fusion = bf16[1536,4096]{1,0:T(8,128)(2,1)} fusion(f32[1536,4096]{1,0:T(8,128)} %fusion.3, bf16[1,352,4096]{2,1,0:T(8,128)(2,1)} %param.14, f32[1536,352]{0,1:T(8,128)} %copy-done.3, f32[1536,352]{0,1:T(8,128)} %copy.63), kind=kOutput, calls=%fused_computation.3 | convolution fusion | flops 4447174656 | bytes 44957696 | tf_op jit(solution)/shard_map/dot_general | solution.py:89
  137.9 1.8 gather_fusion.2
  141.5 4.0 %fusion.18 = bf16[48,96,128]{2,0,1:T(8,128)(2,1)} fusion(bf16[96,48,128]{2,1,0:T(8,128)(2,1)} %gather_fusion.2, bf16[96,48,128]{2,1,0:T(8,128)(2,1)} %gather_fusion.1, pred[96]{0:T(512)(128)(4,1)S(1)} %compare_and_fusion), kind=kLoop, calls=%fused_computation.20 | loop fusion | flops 8257536 | bytes 3539040 | tf_op jit(solution)/shard_map/convert_element_type | solution.py:76
  145.5 5.2 %all-to-all-start.2 = ((bf16[48,96,128]{2,0,1:T(8,128)(2,1)}), bf16[48,96,128]{2,0,1:T(8,128)(2,1)S(1)}, u32[]{:S(2)}, u32[]{:S(2)}) async-start(bf16[48,96,128]{2,0,1:T(8,128)(2,1)} %fusion.18), calls=%async_computation.3 | async-start | bytes 2359296 | tf_op jit(solution)/shard_map/all_to_all | solution.py:77
  151.0 87.4 %reduce-scatter.2.cloned.1.call-done = bf16[48,4096]{1,0:T(8,128)(2,1)} async-done(((bf16[1536,4096]{1,0:T(8,128)(2,1)}), bf16[48,4096]{1,0:T(8,128)(2,1)}) %reduce-scatter.2.cloned.1.call-update) | async-done | bytes 393232 | tf_op jit(solution)/shard_map/reduce_scatter | solution.py:86
  241.0 16.6 %copy.70 = bf16[1,1536,4096]{1,2,0:T(8,128)(2,1)} copy(bf16[1,1536,4096]{2,1,0:T(8,128)(2,1)} %all-gather.3.cloned.1.call-done) | data formatting | bytes 25165824 | tf_op jit(solution)/shard_map/all_gather | solution.py:69
  257.6 16.2 %copy.71 = bf16[1536,32,128]{2,0,1:T(8,128)(2,1)} copy(bf16[1536,32,128]{0,2,1:T(8,128)(2,1)} %bitcast.69) | data formatting | bytes 25165824 | tf_op jit(solution)/shard_map/reshape | solution.py:96
  273.8 6.5 %gather_fusion = bf16[3,1536,128]{2,1,0:T(8,128)(2,1)} fusion(bf16[1536,32,128]{2,0,1:T(8,128)(2,1)} %copy.71, s32[1024]{0:T(1024)S(1)} %pad_clamp_fusion), kind=kCustom, calls=%fused_computation.2 | custom fusion | bytes 2359308 | tf_op jit(solution)/shard_map/jit(_take)/gather | solution.py:96
  280.3 2.9 fusion.45
  (46 shorter events, 11.1 us)
Async XLA Ops:
  7.2 98.5 %copy-start = (bf16[1,352,4096]{2,1,0:T(8,128)(2,1)S(1)}, bf16[1,352,4096]{2,1,0:T(8,128)(2,1)}, u32[]{:S(2)}) copy-start(bf16[1,352,4096]{2,1,0:T(8,128)(2,1)} %param.13) | copy-start | bytes 8650756
  7.2 88.4 %all-gather.3.cloned.1.call-start = ((), (), s32[]{:S(2)}) async-start(), calls=%async_computation.5 | async-start | bytes 12976128 | tf_op jit(solution)/shard_map/all_gather | solution.py:69
  14.4 32.7 %all-to-all-start.1 = ((bf16[48,32,352]{2,0,1:T(8,128)(2,1)}), bf16[48,32,352]{2,0,1:T(8,128)(2,1)}, u32[]{:S(2)}, u32[]{:S(2)}) async-start(bf16[48,32,352]{2,0,1:T(8,128)(2,1)} %copy.59), calls=%async_computation.1 | async-start | bytes 2359296 | tf_op jit(solution)/shard_map/all_to_all | solution.py:67
  47.1 33.2 %all-to-all-start = ((bf16[48,32,352]{2,0,1:T(8,128)(2,1)}), bf16[48,32,352]{2,0,1:T(8,128)(2,1)}, u32[]{:S(2)}, u32[]{:S(2)}) async-start(bf16[48,32,352]{2,0,1:T(8,128)(2,1)} %copy.57), calls=%async_computation | async-start | bytes 2359296 | tf_op jit(solution)/shard_map/all_to_all | solution.py:68
  51.8 186.6 %reduce-scatter.2.cloned.1.call-start = ((), (), s32[]{:S(2)}) async-start(), calls=%async_computation.4 | async-start | bytes 12976128 | tf_op jit(solution)/shard_map/reduce_scatter | solution.py:86
  95.6 10.1 %copy-start.2 = (f32[1536,352]{0,1:T(8,128)S(1)}, f32[1536,352]{0,1:T(8,128)}, u32[]{:S(2)}) copy-start(f32[1536,352]{0,1:T(8,128)} %copy.63) | copy-start | bytes 6488068
  95.6 10.1 %copy-start.4 = (f32[1536,352]{0,1:T(8,128)S(1)}, f32[1536,352]{0,1:T(8,128)}, u32[]{:S(2)}) copy-start(f32[1536,352]{0,1:T(8,128)} %copy.58) | copy-start | bytes 6488068
  104.3 1.4 copy-start.3
  134.5 1.2 copy-start.5
  135.7 1.2 copy-start.6
  137.0 0.7 copy-start.8
  137.0 0.8 copy-start.9
  141.5 9.3 %copy-start.7 = (s32[1,64]{1,0:T(1,128)S(1)}, s32[1,64]{1,0:T(1,128)}, u32[]{:S(2)}) copy-start(s32[1,64]{1,0:T(1,128)} %param.18) | copy-start | bytes 772
  145.5 94.3 %all-to-all-start.2 = ((bf16[48,96,128]{2,0,1:T(8,128)(2,1)}), bf16[48,96,128]{2,0,1:T(8,128)(2,1)S(1)}, u32[]{:S(2)}, u32[]{:S(2)}) async-start(bf16[48,96,128]{2,0,1:T(8,128)(2,1)} %fusion.18), calls=%async_computation.3 | async-start | bytes 2359296 | tf_op jit(solution)/shard_map/all_to_all | solution.py:77
  238.4 44.8 %collective-permute-start = (bf16[48,4096]{1,0:T(8,128)(2,1)}, bf16[48,4096]{1,0:T(8,128)(2,1)S(1)}, u32[]{:S(2)}, u32[]{:S(2)}) collective-permute-start(bf16[48,4096]{1,0:T(8,128)(2,1)} %reduce-scatter.2.cloned.1.call-done), channel_id=1, source_target_pairs={{32,0},{64,32},{96,64},{33,1},{65,33},{97,65},{34,2},{66,34},{98,6... | collective-permute-start | bytes 1179656 | tf_op jit(solution)/shard_map/ppermute | solution.py:12
  273.8 10.1 %copy-start.1 = (bf16[1,352,4096]{2,1,0:T(8,128)(2,1)S(1)}, bf16[1,352,4096]{2,1,0:T(8,128)(2,1)}, u32[]{:S(2)}) copy-start(bf16[1,352,4096]{2,1,0:T(8,128)(2,1)} %param.13) | copy-start | bytes 8650756
Sparse Core Ops, SparseCore 0:
  10.2 85.2 all-gather.2
  134.6 103.7 reduce-scatter.1

commit v2 on v1

v2 whole, which is shorter than its diff:
```python
import jax
import jax.numpy as jnp
from jax import lax
from jax.experimental import pallas as pl
from jax.experimental.pallas import tpu as pltpu
from jax.sharding import PartitionSpec as P

CAP = 3
MESH = pl.DeviceIdType.MESH
BF = jnp.bfloat16
F32 = jnp.float32
SIDE = 4
TOK = 48
WIDTH = 4096
UNITS = 352
WIN = 768
HALF = WIDTH // 2
QUART = WIDTH // 4


def gelu_pair(values):
    coeff = 0.7978845608
    cubic = values * values * values
    tangent = jnp.tanh(coeff * (values + 0.044715 * cubic))
    activated = 0.5 * values * (1.0 + tangent)
    slope = 0.5 * (1.0 + tangent) + 0.5 * values * (1.0 - tangent * tangent) * coeff * (
        1.0 + 3.0 * 0.044715 * values * values
    )
    return (activated, slope)


def owner_slots(owners):
    count_blocks = owners.shape[0]
    same = owners[:, None] == owners[None, :]
    index_list = jnp.arange(count_blocks, dtype=jnp.int32)
    earlier = index_list[None, :] < index_list[:, None]
    return jnp.sum((same & earlier).astype(jnp.int32), axis=1)


def kernel(
    slot_rows, slot_cols, d_out, w_down, w_gate, w_up, gate, up,
    grad_out, block_out,
    wd, wg, wu, x, gp, uq, lg, t, rb, rc, fin, gl, ul, xb, hs, hr, pb, pr,
    loc, w_send, w_recv, ag_send, ag_recv, a2_send, a2_recv, h_send, h_recv,
    rb_send, rb_recv, rc_send, rc_recv, x_send, x_recv, p_send, p_recv,
):
    sec = lax.axis_index("section")
    me = lax.axis_index("dp")
    core = lax.rem(me, 2)
    chip = lax.div(me, 2)
    yy = lax.div(chip, SIDE)
    zz = lax.rem(chip, SIDE)

    def dev(y, z):
        return (sec, (y * SIDE + z) * 2 + core)

    def step(p, by):
        return lax.rem(p + (by + SIDE), SIDE)

    partner = (sec, chip * 2 + (1 - core))
    prev_sec = (lax.rem(sec + 3, 4), me)
    next_sec = (lax.rem(sec + 1, 4), me)
    others = [(i, j) for i in range(SIDE) for j in range(SIDE) if (i, j) != (0, 0)]

    barrier = pltpu.get_barrier_semaphore()
    for dy, dz in others:
        pl.semaphore_signal(barrier, inc=1, device_id=dev(step(yy, dy), step(zz, dz)), device_id_type=MESH)
    for target in (partner, prev_sec, next_sec):
        pl.semaphore_signal(barrier, inc=1, device_id=target, device_id_type=MESH)

    started = []

    def send(src, dst, s_sem, r_sem, target):
        copy = pltpu.make_async_remote_copy(
            src_ref=src, dst_ref=dst, send_sem=s_sem, recv_sem=r_sem,
            device_id=target, device_id_type=MESH,
        )
        copy.start()
        started.append(copy)
        return copy

    pad = 64 * lax.rem(chip, 2)
    place = pl.multiple_of(pad + core * UNITS, 32)
    rows = pl.ds(place, UNITS)
    local = [
        pltpu.make_async_copy(d_out, x.at[yy, zz], loc.at[0]),
        pltpu.make_async_copy(w_down, wd.at[rows], loc.at[3]),
        pltpu.make_async_copy(w_gate, wg.at[rows], loc.at[4]),
        pltpu.make_async_copy(w_up, wu.at[rows], loc.at[5]),
    ]
    for copy in local:
        copy.start()

    def lanes_of(k):
        return pl.ds(pl.multiple_of(k * 128, 128), 128)

    def load_block(k, carry):
        pltpu.make_async_copy(gate.at[:, lanes_of(k)], gl.at[k], loc.at[1]).start()
        pltpu.make_async_copy(up.at[:, lanes_of(k)], ul.at[k], loc.at[2]).start()
        return carry

    lax.fori_loop(0, gl.shape[0], load_block, 0)
    pl.semaphore_wait(barrier, len(others) + 3)

    def along(half, first, by, p, q):
        if (half == 0) == first:
            return dev(step(yy, by), zz)
        return dev(yy, step(zz, by))

    pos = [(yy, zz), (zz, yy)]

    def at(half, p, q):
        return (p, q) if half == 0 else (q, p)

    def cols(half, part=None):
        if part is None:
            return pl.ds(half * HALF, HALF)
        return pl.ds(half * HALF + part * QUART, QUART)

    def piece(half, p, q, part=None):
        a, b = at(half, p, q)
        return x.at[a, b, :, cols(half, part)]

    def ag(half, k, src, dst, target):
        return send(src, dst, ag_send.at[half, k], ag_recv.at[half, k], target)

    got = {}
    near = (0, -1, 1, 2)

    def spread(half, j, from_input=False):
        p, q = pos[half]
        pj = step(p, near[j])
        src = d_out.at[:, cols(half)] if from_input else piece(half, pj, q)
        dst = piece(half, pj, q)
        for n, by in ((0, 1), (1, -1)):
            got[half, 4 + 4 * j + n] = ag(half, 4 + 4 * j + n, src, dst, along(half, False, by, p, q))

    def pass_on(half, j):
        p, q = pos[half]
        pj = step(p, near[j])
        for n, by in ((0, 1), (1, -1)):
            got[half, 4 + 4 * j + n].wait_recv()
            ref = piece(half, pj, step(q, -by), n)
            got[half, 6 + 4 * j + n] = ag(half, 6 + 4 * j + n, ref, ref, along(half, False, by, p, q))

    for half in (0, 1):
        p, q = pos[half]
        for n, by in ((0, 1), (1, -1)):
            got[half, n] = ag(half, n, d_out.at[:, cols(half)], piece(half, p, q), along(half, True, by, p, q))
    w_copies = []
    for n, (src, dst) in enumerate(((w_down, wd), (w_gate, wg), (w_up, wu))):
        w_copies.append(send(src, dst.at[rows], w_send.at[n], w_recv.at[n], partner))
    for half in (0, 1):
        spread(half, 0, True)
    zero_rows = pl.ds(pl.multiple_of(704 - 11 * pad, 64), 64)
    for ref in (wd, wg, wu):
        ref[zero_rows, :] = jnp.zeros((64, WIDTH), BF)

    for n, by in ((0, 1), (1, -1)):
        for half in (0, 1):
            p, q = pos[half]
            got[half, n].wait_recv()
            ref = piece(half, step(p, -by), q, n)
            got[half, 2 + n] = ag(half, 2 + n, ref, ref, along(half, True, by, p, q))
        for half in (0, 1):
            spread(half, 1 + n)
    for half in (0, 1):
        pass_on(half, 0)

    pltpu.make_async_copy(gl, gl, loc.at[1]).wait()
    pltpu.make_async_copy(ul, ul, loc.at[2]).wait()

    def one_slot(s, carry):
        g = gl[slot_rows[s]].astype(F32)
        u = ul[slot_rows[s]].astype(F32)
        hs[lax.div(s, 6), lax.rem(s, 6)] = (gelu_pair(g)[0] * u).astype(BF)
        return carry

    lax.fori_loop(0, 48, one_slot, 0)
    for half in (0, 1):
        got[half, 2].wait_recv()
        got[half, 3].wait_recv()
        spread(half, 3)

    def window(g):
        return pl.ds(pl.multiple_of(lax.div(g * 11, 2) * 128, 128), WIN)

    a2 = []
    for k, (dy, dz) in enumerate(others):
        ty, tz = step(yy, dy), step(zz, dz)
        win = window(ty * SIDE + tz)
        for n, (src, dst) in enumerate(((gate, gp), (up, uq))):
            a2.append(send(src.at[:, win], dst.at[yy, zz], a2_send.at[n, k], a2_recv.at[n, k], dev(ty, tz)))
    mine = window(chip)
    own = [
        pltpu.make_async_copy(gate.at[:, mine], gp.at[yy, zz], loc.at[6]),
        pltpu.make_async_copy(up.at[:, mine], uq.at[yy, zz], loc.at[7]),
    ]
    for copy in own:
        copy.start()
    for half in (0, 1):
        pass_on(half, 1)
        pass_on(half, 2)
    lax.fori_loop(48, 96, one_slot, 0)
    for half in (0, 1):
        pass_on(half, 3)
    for j in range(4):
        for half in (0, 1):
            got[half, 6 + 4 * j].wait_recv()
            got[half, 7 + 4 * j].wait_recv()

    hid = []
    for k, (dy, dz) in enumerate(others):
        ty, tz = step(yy, dy), step(zz, dz)
        hid.append(send(hs.at[ty * SIDE + tz], hr.at[chip], h_send.at[k], h_recv.at[k], dev(ty, tz)))
    own_h = pltpu.make_async_copy(hs.at[chip], hr.at[chip], loc.at[8])
    own_h.start()

    local[0].wait()

    def copy_block(k, carry):
        pltpu.make_async_copy(x.at[:, :, :, lanes_of(k)], xb.at[k], loc.at[9]).start()
        return carry

    lax.fori_loop(0, xb.shape[0], copy_block, 0)
    local[1].wait()
    w_copies[0].wait_recv()

    def dh_tile(i, carry):
        n = lax.div(i, 2)
        m = lax.rem(i, 2)
        units = pl.ds(pl.multiple_of(n * 256, 256), 256)
        a = x[pl.ds(m * 2, 2)].reshape(2 * SIDE * TOK, WIDTH)
        out = lax.dot_general(a, wd[units, :], (((1,), (1,)), ((), ())), preferred_element_type=F32)
        lg[pl.ds(m * 2, 2), :, :, units] = out.astype(BF).reshape(2, SIDE, TOK, 256)
        return carry

    lax.fori_loop(0, 6, dh_tile, 0)

    for copy in own:
        copy.wait()
    for copy in a2:
        copy.wait_recv()

    def point(i, carry):
        a, b = lax.div(i, SIDE), lax.rem(i, SIDE)
        for k in range(WIN // 128):
            lane = pl.ds(k * 128, 128)
            activated, slope = gelu_pair(gp[a, b, :, lane].astype(F32))
            dh = lg[a, b, :, lane].astype(F32)
            u = uq[a, b, :, lane].astype(F32)
            lg[a, b, :, lane] = (dh * u * slope).astype(BF)
            gp[a, b, :, lane] = (dh * activated).astype(BF)
        return carry

    lax.fori_loop(0, SIDE * SIDE, point, 0)
    for n in (2, 3):
        local[n].wait()
    for n in (1, 2):
        w_copies[n].wait_recv()

    def group(half, ref, p, lanes):
        if half == 0:
            return ref[p, :, :, lanes]
        return ref[:, p, :, lanes]

    def put(half, ref, p, lanes, value):
        if half == 0:
            ref[p, :, :, lanes] = value
        else:
            ref[:, p, :, lanes] = value

    def view(half, ref, p, lanes):
        if half == 0:
            return ref.at[p, :, :, lanes]
        return ref.at[:, p, :, lanes]

    def terms(half, targets):
        def tile(i, carry):
            lanes = pl.ds(pl.multiple_of(half * HALF + i * 256, 256), 256)
            every = pl.ds(0, WIN)
            ga = jnp.concatenate([group(half, lg, p, every).reshape(SIDE * TOK, WIN) for p in targets], axis=0)
            ua = jnp.concatenate([group(half, gp, p, every).reshape(SIDE * TOK, WIN) for p in targets], axis=0)
            out = jnp.dot(ga, wg[:, lanes], preferred_element_type=F32)
            out = out + jnp.dot(ua, wu[:, lanes], preferred_element_type=F32)
            out = out.astype(BF)
            for k, p in enumerate(targets):
                part = out[k * SIDE * TOK : (k + 1) * SIDE * TOK]
                put(half, t, p, lanes, part.reshape(SIDE, TOK, 256))
            return carry

        lax.fori_loop(0, HALF // 256, tile, 0)

    r1 = {}

    def rs1(half, k, p_of, part, by):
        p, q = pos[half]
        r1[half, k] = send(
            view(half, t, p_of, cols(half, part)), rb.at[half, k],
            rb_send.at[half, k], rb_recv.at[half, k], along(half, True, by, p, q),
        )

    for half in (0, 1):
        p, q = pos[half]
        terms(half, [step(p, 2)])
        rs1(half, 0, step(p, 2), 0, 1)
        rs1(half, 1, step(p, 2), 1, -1)
    for half in (0, 1):
        p, q = pos[half]
        terms(half, [step(p, 1), step(p, -1)])
        rs1(half, 2, step(p, 1), 1, 1)
        rs1(half, 3, step(p, -1), 0, -1)

    def add_rows(half, dst_p, part, bufs):
        lanes = cols(half, part)

        def row(i, carry):
            if half == 0:
                total = t[dst_p, i, :, lanes].astype(F32)
            else:
                total = t[i, dst_p, :, lanes].astype(F32)
            for k in bufs:
                total = total + rb[half, k, i].astype(F32)
            if half == 0:
                t[dst_p, i, :, lanes] = total.astype(BF)
            else:
                t[i, dst_p, :, lanes] = total.astype(BF)
            return carry

        lax.fori_loop(0, SIDE, row, 0)

    for half in (0, 1):
        p, q = pos[half]
        r1[half, 0].wait_recv()
        add_rows(half, step(p, 1), 0, (0,))
        rs1(half, 4, step(p, 1), 0, 1)
        r1[half, 1].wait_recv()
        add_rows(half, step(p, -1), 1, (1,))
        rs1(half, 5, step(p, -1), 1, -1)
    for half in (0, 1):
        terms(half, [pos[half][0]])

    own_h.wait()
    for copy in hid:
        copy.wait_recv()
    pltpu.make_async_copy(xb, xb, loc.at[9]).wait()
    for s in range(6):
        h = hr[:, s].reshape(SIDE * SIDE * TOK, 128)
        d = xb[slot_cols[s]].reshape(SIDE * SIDE * TOK, 128)
        pb[s] = lax.dot_general(h, d, (((0,), (0,)), ((), ())), preferred_element_type=F32)
    p_copy = send(pb.at[pl.ds((1 - core) * CAP, CAP)], pr, p_send.at[0], p_recv.at[0], partner)

    r2 = {}

    def piece_t(half, q_of, part):
        a, b = at(half, pos[half][0], q_of)
        return (a, b, slice(None), cols(half, part))

    def rs2(half, k, q_of, part, by):
        p, q = pos[half]
        r2[half, k] = send(
            t.at[piece_t(half, q_of, part)], rc.at[half, k],
            rc_send.at[half, k], rc_recv.at[half, k], along(half, False, by, p, q),
        )

    for half in (0, 1):
        p, q = pos[half]
        for k in (2, 3, 4, 5):
            r1[half, k].wait_recv()
        add_rows(half, p, 0, (3, 4))
        add_rows(half, p, 1, (2, 5))
        rs2(half, 0, step(q, 2), 0, 1)
        rs2(half, 1, step(q, 2), 1, -1)
        rs2(half, 2, step(q, 1), 1, 1)
        rs2(half, 3, step(q, -1), 0, -1)
    for half in (0, 1):
        p, q = pos[half]
        for k, by in ((0, 1), (1, -1)):
            r2[half, k].wait_recv()
            here = piece_t(half, step(q, by), k)
            t[here] = (t[here].astype(F32) + rc[half, k].astype(F32)).astype(BF)
            rs2(half, 4 + k, step(q, by), k, by)
    last = []
    for half in (0, 1):
        p, q = pos[half]
        for k in (2, 3, 4, 5):
            r2[half, k].wait_recv()
        for part, bufs in ((0, (3, 4)), (1, (2, 5))):
            total = t[piece_t(half, q, part)].astype(F32)
            for k in bufs:
                total = total + rc[half, k].astype(F32)
            fin[:, cols(half, part)] = total.astype(BF)
        last.append(send(
            fin.at[:, cols(half)], grad_out.at[:, cols(half)],
            x_send.at[half], x_recv.at[half], prev_sec,
        ))
    p_copy.wait_recv()
    block_out[...] = ((pb[pl.ds(core * CAP, CAP)] + pr[...]) * (1.0 / 32.0)).astype(BF)
    for copy in last:
        copy.wait_recv()
    for copy in started:
        copy.wait_send()


def shards(d_out, down_weight, gate_weight, up_weight, gate_pre, up_val, block_rows, block_cols, block_owner):
    row_ids, col_ids, owners = block_rows[0], block_cols[0], block_owner[0]
    replicas = lax.axis_size("dp")
    position = owners * CAP + owner_slots(owners)
    slot_ids = jnp.arange(replicas * CAP, dtype=jnp.int32)
    match = position[None, :] == slot_ids[:, None]
    slot_rows = jnp.sum(jnp.where(match, row_ids[None, :], 0), axis=1)
    me = lax.axis_index("dp")
    chip_slots = (me // 2) * (2 * CAP) + jnp.arange(2 * CAP, dtype=jnp.int32)
    slot_cols = jnp.sum(jnp.where(position[None, :] == chip_slots[:, None], col_ids[None, :], 0), axis=1)
    my_slots = me * CAP + jnp.arange(CAP, dtype=jnp.int32)
    present = jnp.any(position[None, :] == my_slots[:, None], axis=1)

    smem = pl.BlockSpec(memory_space=pltpu.SMEM)
    hbm = pl.BlockSpec(memory_space=pl.ANY)
    dma = pltpu.SemaphoreType.DMA
    grid_shape = (SIDE, SIDE, TOK)
    grad, blocks = pl.pallas_call(
        kernel,
        out_shape=(
            jax.ShapeDtypeStruct((TOK, WIDTH), BF),
            jax.ShapeDtypeStruct((CAP, 128, 128), BF),
        ),
        in_specs=[smem, smem] + [hbm] * 6,
        out_specs=(hbm, pl.BlockSpec(memory_space=pltpu.VMEM)),
        scratch_shapes=[
            pltpu.VMEM((WIN, WIDTH), BF),
            pltpu.VMEM((WIN, WIDTH), BF),
            pltpu.VMEM((WIN, WIDTH), BF),
            pltpu.VMEM((*grid_shape, WIDTH), BF),
            pltpu.VMEM((*grid_shape, WIN), BF),
            pltpu.VMEM((*grid_shape, WIN), BF),
            pltpu.VMEM((*grid_shape, WIN), BF),
            pltpu.VMEM((*grid_shape, WIDTH), BF),
            pltpu.VMEM((2, 6, SIDE, TOK, QUART), BF),
            pltpu.VMEM((2, 6, TOK, QUART), BF),
            pltpu.VMEM((TOK, WIDTH), BF),
            pltpu.VMEM((88, TOK, 128), BF),
            pltpu.VMEM((88, TOK, 128), BF),
            pltpu.VMEM((32, *grid_shape, 128), BF),
            pltpu.VMEM((16, 6, TOK, 128), BF),
            pltpu.VMEM((16, 6, TOK, 128), BF),
            pltpu.VMEM((6, 128, 128), F32),
            pltpu.VMEM((CAP, 128, 128), F32),
            dma((10,)),
            dma((3,)), dma((3,)),
            dma((2, 20)), dma((2, 20)),
            dma((2, 15)), dma((2, 15)),
            dma((15,)), dma((15,)),
            dma((2, 6)), dma((2, 6)),
            dma((2, 6)), dma((2, 6)),
            dma((2,)), dma((2,)),
            dma((1,)), dma((1,)),
        ],
        compiler_params=pltpu.CompilerParams(
            collective_id=0, has_side_effects=True, vmem_limit_bytes=62 * 1024 * 1024
        ),
        name="relay",
    )(slot_rows, slot_cols, d_out[0], down_weight[0], gate_weight[0], up_weight[0], gate_pre[0], up_val[0])
    last = lax.axis_index("section") == lax.axis_size("section") - 1
    grad = jnp.where(last, jnp.zeros((), BF), grad)
    result = jnp.where(present[:, None, None], blocks, jnp.zeros((), BF))
    return (grad[None], result[None])


def solution(mesh):
    return jax.shard_map(
        shards,
        mesh=mesh,
        in_specs=(P("section", "dp", None),) * 6 + (P("section", None),) * 3,
        out_specs=(P("section", "dp", None), P("section", "dp", None, None)),
        check_vma=False,
    )
```

time: 294 us -> 143 us (0.49)
  waiting for transfers between devices: 137 us -> 0 us
  Pallas kernels: 0 us -> 133 us
  local copies, waits for them, and re-layouts: 68.6 us -> 0 us
  matrix products: 40.4 us -> 0 us
  starting transfers between devices: 20 us -> 0 us
  between operations: 14.2 us -> 0.68 us
    pallas_call x0 -> x1, Pallas kernels: none -> 133 us  [shards(): pl.pallas_call(kernel, out_shape=(jax.ShapeDtypeStruct((TOK, WIDTH), BF),...]
    reduce_scatter x1 -> x0, waiting for transfers between devices: 87.4 us -> none  [shards(): lax.psum_scatter((jnp.dot(local_gate, w_gate, preferred_element_type=jnp....]
    dot_general x4 -> x0, matrix products: 40.4 us -> none  [the longest x1 16.5 us: shards(): jnp.dot(local_up, w_up, preferred_element_type=jnp.float32)]
    all_to_all x3 -> x0, waiting for transfers between devices: 39.7 us -> none  [the longest x1 21.9 us: shards(): lax.all_to_all(up_local, 'dp', split_axis=1, concat_axis=0, tiled=True)]
    all_to_all x3 -> x0, starting transfers between devices: 18.5 us -> none  [the longest x1 8.56 us: shards(): lax.all_to_all(gate_local, 'dp', split_axis=1, concat_axis=0, tiled=True)]
    all_gather x1 -> x0, local copies, waits for them, and re-layouts: 16.6 us -> none  [shards(): every_row = lax.all_gather(grad_rows, 'dp', axis=0, tiled=True)]
    reshape x1 -> x0, local copies, waits for them, and re-layouts: 16.2 us -> none  [shards(): every_row.reshape(every_row.shape[0], -1, 128)]
    all_to_all x5 -> x0, local copies, waits for them, and re-layouts: 13.9 us -> none  [the longest x2 6.46 us: shards(): lax.all_to_all(gate_local, 'dp', split_axis=1, concat_axis=0, tiled=True)]
  transfers between devices with their start and end apart: 6 -> 0, of which waited for: 4 -> 0; matrix products, arithmetic and copies ran while one was open for 24% -> 0% of each run, Pallas kernels for 0% -> 0%
where the time goes in v2:
time: 143 us; the launch traced here: 142 us
  Pallas kernels  133 us (93%)
  other arithmetic  7.77 us (5%)
    pallas_call x1, Pallas kernels, shards(): pl.pallas_call(kernel, out_shape=(jax.ShapeDtypeStruct((TOK, WIDTH), BF),...  133 us
    broadcast_in_dim x2, other arithmetic, shards(): return (grad[None], result[None])  3.39 us

profile of v2, /device:TPU:0, one launch (start us, length us, event | category | flops | bytes accessed | tf_op | source)
XLA Modules:
  0.0 141.8 jit_solution(4988016050454312541)
XLA Ops:
  0.7 0.9 convert_reduce_fusion
  1.6 0.7 fusion.1
  2.2 0.2 compare_reduce_fusion
  2.4 1.3 select_reduce_fusion.1.slot_cols
  3.8 1.3 select_reduce_fusion.slot_rows
  5.0 133.3 %relay.1 = (bf16[48,4096]{1,0:T(8,128)(2,1)}, bf16[3,128,128]{2,1,0:T(8,128)(2,1)}) custom-call(s32[96]{0:T(128)} %select_reduce_fusion.slot_rows, s32[6]{0:T(128)} %select_reduce_fusion.1.slot_cols, bf16[48,4096]{1,0:T(8,128)(2,1)} %bitcast.24, bf16[352,4096]{1,0:T(8,128)(2,1)} %bitcast.19, bf16[352,4096]{1,0:T(8,128)(2,1)} %bitcast.20, ...), custom_call_target="tpu_custom_call" | custom-call | tf_op jit(solution)/shard_map/relay/pallas_call | solution.py:422
  138.4 1.8 %select_bitcast_fusion = bf16[1,48,4096]{2,1,0:T(8,128)(2,1)} fusion(bf16[48,4096]{1,0:T(8,128)(2,1)} %get-tuple-element.4, pred[]{:T(512)S(6)} %eq.59), kind=kLoop, calls=%fused_computation | loop fusion | flops 196608 | bytes 786433 | tf_op jit(solution)/shard_map/broadcast_in_dim | solution.py:467
  140.1 1.6 %select_bitcast_fusion.1 = bf16[1,3,128,128]{3,2,1,0:T(8,128)(2,1)} fusion(bf16[3,128,128]{2,1,0:T(8,128)(2,1)} %get-tuple-element.5, pred[3]{0:T(512)(128)(4,1)S(1)} %compare_reduce_fusion), kind=kLoop, calls=%fused_computation.1 | loop fusion | flops 49152 | bytes 196611 | tf_op jit(solution)/shard_map/broadcast_in_dim | solution.py:467
  (2 shorter events, 0.0 us)

commit v3 on v2

--- a/solution.py
+++ b/solution.py
@@ -16,6 +16,7 @@
 WIN = 768
 HALF = WIDTH // 2
 QUART = WIDTH // 4
+CHUNKS = ((0, 1280), (1280, 768))
 
 
 def gelu_pair(values):
@@ -29,18 +30,10 @@
     return (activated, slope)
 
 
-def owner_slots(owners):
-    count_blocks = owners.shape[0]
-    same = owners[:, None] == owners[None, :]
-    index_list = jnp.arange(count_blocks, dtype=jnp.int32)
-    earlier = index_list[None, :] < index_list[:, None]
-    return jnp.sum((same & earlier).astype(jnp.int32), axis=1)
-
-
 def kernel(
-    slot_rows, slot_cols, d_out, w_down, w_gate, w_up, gate, up,
+    block_rows, block_cols, block_owner, d_out, w_down, w_gate, w_up, gate, up,
     grad_out, block_out,
-    wd, wg, wu, x, gp, uq, lg, t, rb, rc, fin, gl, ul, xb, hs, hr, pb, pr,
+    wd, wg, wu, x, gp, uq, lg, t, rb, rc, fin, gl, ul, xb, hs, hr, pb, pr, tab, slots,
     loc, w_send, w_recv, ag_send, ag_recv, a2_send, a2_recv, h_send, h_recv,
     rb_send, rb_recv, rc_send, rc_recv, x_send, x_recv, p_send, p_recv,
 ):
@@ -61,6 +54,7 @@
     prev_sec = (lax.rem(sec + 3, 4), me)
     next_sec = (lax.rem(sec + 1, 4), me)
     others = [(i, j) for i in range(SIDE) for j in range(SIDE) if (i, j) != (0, 0)]
+    others.sort(key=lambda d: -(min(d[0], SIDE - d[0]) + min(d[1], SIDE - d[1])))
 
     barrier = pltpu.get_barrier_semaphore()
     for dy, dz in others:
@@ -167,12 +161,30 @@
     for half in (0, 1):
         pass_on(half, 0)
 
+    blocks = block_owner.shape[1]
+    row_id = lax.broadcasted_iota(jnp.int32, (blocks, blocks), 0)
+    col_id = lax.broadcasted_iota(jnp.int32, (blocks, blocks), 1)
+
+    def upright(ref):
+        wide = jnp.broadcast_to(ref[...], (blocks, blocks))
+        return jnp.sum(jnp.where(row_id == col_id, wide, 0), axis=1, keepdims=True)
+
+    owner = upright(block_owner)
+    earlier = (block_owner[...] == owner) & (col_id < row_id)
+    position = owner * CAP + jnp.sum(jnp.where(earlier, 1, 0), axis=1, keepdims=True)
+    match = position == lax.broadcasted_iota(jnp.int32, (blocks, 128), 1)
+    for k, value in enumerate((upright(block_rows), upright(block_cols), jnp.ones((blocks, 1), jnp.int32))):
+        tab[k : k + 1, :] = jnp.sum(jnp.where(match, value, 0), axis=0, keepdims=True)
+    tables = pltpu.make_async_copy(tab, slots, loc.at[10])
+    tables.start()
+    tables.wait()
+
     pltpu.make_async_copy(gl, gl, loc.at[1]).wait()
     pltpu.make_async_copy(ul, ul, loc.at[2]).wait()
 
     def one_slot(s, carry):
-        g = gl[slot_rows[s]].astype(F32)
-        u = ul[slot_rows[s]].astype(F32)
+        g = gl[slots[0, s]].astype(F32)
+        u = ul[slots[0, s]].astype(F32)
         hs[lax.div(s, 6), lax.rem(s, 6)] = (gelu_pair(g)[0] * u).astype(BF)
         return carry
 
@@ -186,10 +198,10 @@
         return pl.ds(pl.multiple_of(lax.div(g * 11, 2) * 128, 128), WIN)
 
     a2 = []
-    for k, (dy, dz) in enumerate(others):
-        ty, tz = step(yy, dy), step(zz, dz)
-        win = window(ty * SIDE + tz)
-        for n, (src, dst) in enumerate(((gate, gp), (up, uq))):
+    for n, (src, dst) in enumerate(((gate, gp), (up, uq))):
+        for k, (dy, dz) in enumerate(others):
+            ty, tz = step(yy, dy), step(zz, dz)
+            win = window(ty * SIDE + tz)
             a2.append(send(src.at[:, win], dst.at[yy, zz], a2_send.at[n, k], a2_recv.at[n, k], dev(ty, tz)))
     mine = window(chip)
     own = [
@@ -275,9 +287,11 @@
             return ref.at[p, :, :, lanes]
         return ref.at[:, p, :, lanes]
 
-    def terms(half, targets):
+    def terms(half, c, targets):
+        first, width = CHUNKS[c]
+
         def tile(i, carry):
-            lanes = pl.ds(pl.multiple_of(half * HALF + i * 256, 256), 256)
+            lanes = pl.ds(pl.multiple_of(half * HALF + first + i * 256, 256), 256)
             every = pl.ds(0, WIN)
             ga = jnp.concatenate([group(half, lg, p, every).reshape(SIDE * TOK, WIN) for p in targets], axis=0)
             ua = jnp.concatenate([group(half, gp, p, every).reshape(SIDE * TOK, WIN) for p in targets], axis=0)
@@ -289,30 +303,28 @@
                 put(half, t, p, lanes, part.reshape(SIDE, TOK, 256))
             return carry
 
-        lax.fori_loop(0, HALF // 256, tile, 0)
-
-    r1 = {}
-
-    def rs1(half, k, p_of, part, by):
+        lax.fori_loop(0, width // 256, tile, 0)
+
+    def lanes_at(half, c, part):
+        first, width = CHUNKS[c]
+        return pl.ds(half * HALF + first + part * (width // 2), width // 2)
+
+    def held(c):
+        first, width = CHUNKS[c]
+        return pl.ds(first // 2, width // 2)
+
+    r1, r2 = {}, {}
+
+    def rs1(half, c, k, by, part):
         p, q = pos[half]
-        r1[half, k] = send(
-            view(half, t, p_of, cols(half, part)), rb.at[half, k],
-            rb_send.at[half, k], rb_recv.at[half, k], along(half, True, by, p, q),
+        p_of = step(p, 2) if k < 2 else step(p, by)
+        r1[half, c, k] = send(
+            view(half, t, p_of, lanes_at(half, c, part)), rb.at[half, k, :, :, held(c)],
+            rb_send.at[half, 6 * c + k], rb_recv.at[half, 6 * c + k], along(half, True, by, p, q),
         )
 
-    for half in (0, 1):
-        p, q = pos[half]
-        terms(half, [step(p, 2)])
-        rs1(half, 0, step(p, 2), 0, 1)
-        rs1(half, 1, step(p, 2), 1, -1)
-    for half in (0, 1):
-        p, q = pos[half]
-        terms(half, [step(p, 1), step(p, -1)])
-        rs1(half, 2, step(p, 1), 1, 1)
-        rs1(half, 3, step(p, -1), 0, -1)
-
-    def add_rows(half, dst_p, part, bufs):
-        lanes = cols(half, part)
+    def add_rows(half, c, dst_p, part, bufs):
+        lanes = lanes_at(half, c, part)
 
         def row(i, carry):
             if half == 0:
@@ -320,7 +332,7 @@
             else:
                 total = t[i, dst_p, :, lanes].astype(F32)
             for k in bufs:
-                total = total + rb[half, k, i].astype(F32)
+                total = total + rb[half, k, i, :, held(c)].astype(F32)
             if half == 0:
                 t[dst_p, i, :, lanes] = total.astype(BF)
             else:
@@ -329,16 +341,92 @@
 
         lax.fori_loop(0, SIDE, row, 0)
 
-    for half in (0, 1):
+    def far(c):
+        for half in (0, 1):
+            terms(half, c, [step(pos[half][0], 2)])
+            rs1(half, c, 0, 1, 0)
+            rs1(half, c, 1, -1, 1)
+
+    def near_terms(c):
+        for half in (0, 1):
+            p, q = pos[half]
+            terms(half, c, [step(p, 1), step(p, -1)])
+            rs1(half, c, 2, 1, 1)
+            rs1(half, c, 3, -1, 0)
+
+    def own_terms(c):
+        for half in (0, 1):
+            terms(half, c, [pos[half][0]])
+
+    def relay(c):
+        for k, by in ((0, 1), (1, -1)):
+            for half in (0, 1):
+                r1[half, c, k].wait_recv()
+                add_rows(half, c, step(pos[half][0], by), k, (k,))
+                rs1(half, c, 4 + k, by, k)
+
+    def piece_t(half, c, q_of, part):
+        a, b = at(half, pos[half][0], q_of)
+        return (a, b, slice(None), lanes_at(half, c, part))
+
+    def rs2(half, c, k, q_of, part, by):
         p, q = pos[half]
-        r1[half, 0].wait_recv()
-        add_rows(half, step(p, 1), 0, (0,))
-        rs1(half, 4, step(p, 1), 0, 1)
-        r1[half, 1].wait_recv()
-        add_rows(half, step(p, -1), 1, (1,))
-        rs1(half, 5, step(p, -1), 1, -1)
-    for half in (0, 1):
-        terms(half, [pos[half][0]])
+        r2[half, c, k] = send(
+            t.at[piece_t(half, c, q_of, part)], rc.at[half, k, :, held(c)],
+            rc_send.at[half, 6 * c + k], rc_recv.at[half, 6 * c + k], along(half, False, by, p, q),
+        )
+
+    def turn(c):
+        for half in (0, 1):
+            p, q = pos[half]
+            for k in (2, 3, 4, 5):
+                r1[half, c, k].wait_recv()
+            add_rows(half, c, p, 0, (3, 4))
+            add_rows(half, c, p, 1, (2, 5))
+            rs2(half, c, 0, step(q, 2), 0, 1)
+            rs2(half, c, 1, step(q, 2), 1, -1)
+            rs2(half, c, 2, step(q, 1), 1, 1)
+            rs2(half, c, 3, step(q, -1), 0, -1)
+
+    def relay2(c):
+        for k, by in ((0, 1), (1, -1)):
+            for half in (0, 1):
+                q = pos[half][1]
+                r2[half, c, k].wait_recv()
+                here = piece_t(half, c, step(q, by), k)
+                t[here] = (t[here].astype(F32) + rc[half, k, :, held(c)].astype(F32)).astype(BF)
+                rs2(half, c, 4 + k, step(q, by), k, by)
+
+    kept = jnp.minimum(sec, 1).astype(F32)
+    last = []
+
+    def finish(c):
+        first, width = CHUNKS[c]
+        for half in (0, 1):
+            p, q = pos[half]
+            for k in (2, 3, 4, 5):
+                r2[half, c, k].wait_recv()
+            for part, bufs in ((0, (3, 4)), (1, (2, 5))):
+                total = t[piece_t(half, c, q, part)].astype(F32)
+                for k in bufs:
+                    total = total + rc[half, k, :, held(c)].astype(F32)
+                fin[:, lanes_at(half, c, part)] = (total * kept).astype(BF)
+            lanes = pl.ds(half * HALF + first, width)
+            last.append(send(
+                fin.at[:, lanes], grad_out.at[:, lanes],
+                x_send.at[half, c], x_recv.at[half, c], prev_sec,
+            ))
+
+    far(0)
+    near_terms(0)
+    far(1)
+    relay(0)
+    own_terms(0)
+    near_terms(1)
+    own_terms(1)
+    turn(0)
+    relay(1)
+    relay2(0)
 
     own_h.wait()
     for copy in hid:
@@ -346,56 +434,18 @@
     pltpu.make_async_copy(xb, xb, loc.at[9]).wait()
     for s in range(6):
         h = hr[:, s].reshape(SIDE * SIDE * TOK, 128)
-        d = xb[slot_cols[s]].reshape(SIDE * SIDE * TOK, 128)
+        d = xb[slots[1, chip * 6 + s]].reshape(SIDE * SIDE * TOK, 128)
         pb[s] = lax.dot_general(h, d, (((0,), (0,)), ((), ())), preferred_element_type=F32)
     p_copy = send(pb.at[pl.ds((1 - core) * CAP, CAP)], pr, p_send.at[0], p_recv.at[0], partner)
 
-    r2 = {}
-
-    def piece_t(half, q_of, part):
-        a, b = at(half, pos[half][0], q_of)
-        return (a, b, slice(None), cols(half, part))
-
-    def rs2(half, k, q_of, part, by):
-        p, q = pos[half]
-        r2[half, k] = send(
-            t.at[piece_t(half, q_of, part)], rc.at[half, k],
-            rc_send.at[half, k], rc_recv.at[half, k], along(half, False, by, p, q),
-        )
-
-    for half in (0, 1):
-        p, q = pos[half]
-        for k in (2, 3, 4, 5):
-            r1[half, k].wait_recv()
-        add_rows(half, p, 0, (3, 4))
-        add_rows(half, p, 1, (2, 5))
-        rs2(half, 0, step(q, 2), 0, 1)
-        rs2(half, 1, step(q, 2), 1, -1)
-        rs2(half, 2, step(q, 1), 1, 1)
-        rs2(half, 3, step(q, -1), 0, -1)
-    for half in (0, 1):
-        p, q = pos[half]
-        for k, by in ((0, 1), (1, -1)):
-            r2[half, k].wait_recv()
-            here = piece_t(half, step(q, by), k)
-            t[here] = (t[here].astype(F32) + rc[half, k].astype(F32)).astype(BF)
-            rs2(half, 4 + k, step(q, by), k, by)
-    last = []
-    for half in (0, 1):
-        p, q = pos[half]
-        for k in (2, 3, 4, 5):
-            r2[half, k].wait_recv()
-        for part, bufs in ((0, (3, 4)), (1, (2, 5))):
-            total = t[piece_t(half, q, part)].astype(F32)
-            for k in bufs:
-                total = total + rc[half, k].astype(F32)
-            fin[:, cols(half, part)] = total.astype(BF)
-        last.append(send(
-            fin.at[:, cols(half)], grad_out.at[:, cols(half)],
-            x_send.at[half], x_recv.at[half], prev_sec,
-        ))
+    finish(0)
+    turn(1)
+    relay2(1)
+    finish(1)
     p_copy.wait_recv()
-    block_out[...] = ((pb[pl.ds(core * CAP, CAP)] + pr[...]) * (1.0 / 32.0)).astype(BF)
+    for k in range(CAP):
+        present = slots[2, me * CAP + k].astype(F32)
+        block_out[k] = ((pb[core * CAP + k] + pr[k]) * ((1.0 / 32.0) * present)).astype(BF)
     for copy in last:
         copy.wait_recv()
     for copy in started:
@@ -403,19 +453,7 @@
 
 
 def shards(d_out, down_weight, gate_weight, up_weight, gate_pre, up_val, block_rows, block_cols, block_owner):
-    row_ids, col_ids, owners = block_rows[0], block_cols[0], block_owner[0]
-    replicas = lax.axis_size("dp")
-    position = owners * CAP + owner_slots(owners)
-    slot_ids = jnp.arange(replicas * CAP, dtype=jnp.int32)
-    match = position[None, :] == slot_ids[:, None]
-    slot_rows = jnp.sum(jnp.where(match, row_ids[None, :], 0), axis=1)
-    me = lax.axis_index("dp")
-    chip_slots = (me // 2) * (2 * CAP) + jnp.arange(2 * CAP, dtype=jnp.int32)
-    slot_cols = jnp.sum(jnp.where(position[None, :] == chip_slots[:, None], col_ids[None, :], 0), axis=1)
-    my_slots = me * CAP + jnp.arange(CAP, dtype=jnp.int32)
-    present = jnp.any(position[None, :] == my_slots[:, None], axis=1)
-
-    smem = pl.BlockSpec(memory_space=pltpu.SMEM)
+    vmem = pl.BlockSpec(memory_space=pltpu.VMEM)
     hbm = pl.BlockSpec(memory_space=pl.ANY)
     dma = pltpu.SemaphoreType.DMA
     grid_shape = (SIDE, SIDE, TOK)
@@ -425,8 +463,8 @@
             jax.ShapeDtypeStruct((TOK, WIDTH), BF),
             jax.ShapeDtypeStruct((CAP, 128, 128), BF),
         ),
-        in_specs=[smem, smem] + [hbm] * 6,
-        out_specs=(hbm, pl.BlockSpec(memory_space=pltpu.VMEM)),
+        in_specs=[vmem] * 3 + [hbm] * 6,
+        out_specs=(hbm, vmem),
         scratch_shapes=[
             pltpu.VMEM((WIN, WIDTH), BF),
             pltpu.VMEM((WIN, WIDTH), BF),
@@ -446,25 +484,24 @@
             pltpu.VMEM((16, 6, TOK, 128), BF),
             pltpu.VMEM((6, 128, 128), F32),
             pltpu.VMEM((CAP, 128, 128), F32),
-            dma((10,)),
+            pltpu.VMEM((8, 128), jnp.int32),
+            pltpu.SMEM((8, 128), jnp.int32),
+            dma((11,)),
             dma((3,)), dma((3,)),
             dma((2, 20)), dma((2, 20)),
             dma((2, 15)), dma((2, 15)),
             dma((15,)), dma((15,)),
-            dma((2, 6)), dma((2, 6)),
-            dma((2, 6)), dma((2, 6)),
-            dma((2,)), dma((2,)),
+            dma((2, 12)), dma((2, 12)),
+            dma((2, 12)), dma((2, 12)),
+            dma((2, 2)), dma((2, 2)),
             dma((1,)), dma((1,)),
         ],
         compiler_params=pltpu.CompilerParams(
             collective_id=0, has_side_effects=True, vmem_limit_bytes=62 * 1024 * 1024
         ),
         name="relay",
-    )(slot_rows, slot_cols, d_out[0], down_weight[0], gate_weight[0], up_weight[0], gate_pre[0], up_val[0])
-    last = lax.axis_index("section") == lax.axis_size("section") - 1
-    grad = jnp.where(last, jnp.zeros((), BF), grad)
-    result = jnp.where(present[:, None, None], blocks, jnp.zeros((), BF))
-    return (grad[None], result[None])
+    )(block_rows, block_cols, block_owner, d_out[0], down_weight[0], gate_weight[0], up_weight[0], gate_pre[0], up_val[0])
+    return (grad[None], blocks[None])
 
 
 def solution(mesh):

time: 143 us -> 130 us (0.909)
  other arithmetic: 7.77 us -> 0 us
  Pallas kernels: 133 us -> 126 us
  local copies, waits for them, and re-layouts: 0 us -> 3.31 us
    pallas_call x1, Pallas kernels: 133 us -> 126 us  [shards(): pl.pallas_call(kernel, out_shape=(jax.ShapeDtypeStruct((TOK, WIDTH), BF),...]
    reduce_sum x3 -> x0, other arithmetic: 3.52 us -> none  [the longest x1 1.35 us: shards(): jnp.sum(jnp.where(position[None, :] == chip_slots[:, None], col_ids[None,...]
    broadcast_in_dim x2 -> x0, other arithmetic: 3.39 us -> none  [shards(): return (grad[None], result[None])]
    unnamed x0 -> x2, local copies, waits for them, and re-layouts: none -> 3.31 us
where the time goes in v3:
time: 130 us
  Pallas kernels  126 us (97%)
  local copies, waits for them, and re-layouts  3.31 us (3%)
    pallas_call x1, Pallas kernels, shards(): pl.pallas_call(kernel, out_shape=(jax.ShapeDtypeStruct((TOK, WIDTH), BF),...  126 us
    unnamed x2, local copies, waits for them, and re-layouts  3.31 us

profile of v3, /device:TPU:0, one launch (start us, length us, event | category | flops | bytes accessed | tf_op | source)
XLA Modules:
  0.0 130.0 jit_solution(11184817847489334406)
XLA Ops:
  0.6 126.0 %relay.1 = (bf16[48,4096]{1,0:T(8,128)(2,1)}, bf16[3,128,128]{2,1,0:T(8,128)(2,1)}) custom-call(s32[1,64]{1,0:T(1,128)} %block_rows.1, s32[1,64]{1,0:T(1,128)} %block_cols.1, s32[1,64]{1,0:T(1,128)} %block_owner.1, bf16[48,4096]{1,0:T(8,128)(2,1)} %bitcast.13, bf16[352,4096]{1,0:T(8,128)(2,1)} %bitcast.8, bf16[352,4096]{1,0:T(8,128)(2,1)} %bitcast.9, ...), custom_call_target="tpu_custom_call" | custom-call | tf_op jit(solution)/shard_map/relay/pallas_call | solution.py:460
  126.7 1.8 %copy.13 = bf16[1,48,4096]{2,1,0:T(8,128)(2,1)} copy(bf16[1,48,4096]{2,1,0:T(8,128)(2,1)} %bitcast.14) | data formatting | bytes 786432
  128.4 1.5 %copy.14 = bf16[1,3,128,128]{3,2,1,0:T(8,128)(2,1)} copy(bf16[1,3,128,128]{3,2,1,0:T(8,128)(2,1)} %bitcast.15) | data formatting | bytes 196608

commit v4 on v3

--- a/solution.py
+++ b/solution.py
@@ -16,7 +16,8 @@
 WIN = 768
 HALF = WIDTH // 2
 QUART = WIDTH // 4
-CHUNKS = ((0, 1280), (1280, 768))
+CHUNKS = ((0, 1024), (1024, 768), (1792, 256))
+LAST = len(CHUNKS) - 1
 
 
 def gelu_pair(values):
@@ -54,7 +55,8 @@
     prev_sec = (lax.rem(sec + 3, 4), me)
     next_sec = (lax.rem(sec + 1, 4), me)
     others = [(i, j) for i in range(SIDE) for j in range(SIDE) if (i, j) != (0, 0)]
-    others.sort(key=lambda d: -(min(d[0], SIDE - d[0]) + min(d[1], SIDE - d[1])))
+    others.sort(key=lambda d: (2 not in d, -(min(d[0], SIDE - d[0]) + min(d[1], SIDE - d[1]))))
+    n_far = sum(2 in d for d in others)
 
     barrier = pltpu.get_barrier_semaphore()
     for dy, dz in others:
@@ -194,15 +196,22 @@
         got[half, 3].wait_recv()
         spread(half, 3)
 
+    for half in (0, 1):
+        pass_on(half, 1)
+        pass_on(half, 2)
+    lax.fori_loop(48, 96, one_slot, 0)
+    for half in (0, 1):
+        pass_on(half, 3)
     def window(g):
         return pl.ds(pl.multiple_of(lax.div(g * 11, 2) * 128, 128), WIN)
 
     a2 = []
-    for n, (src, dst) in enumerate(((gate, gp), (up, uq))):
-        for k, (dy, dz) in enumerate(others):
-            ty, tz = step(yy, dy), step(zz, dz)
-            win = window(ty * SIDE + tz)
-            a2.append(send(src.at[:, win], dst.at[yy, zz], a2_send.at[n, k], a2_recv.at[n, k], dev(ty, tz)))
+    for some in (range(n_far), range(n_far, len(others))):
+        for n, (src, dst) in enumerate(((gate, gp), (up, uq))):
+            for k in some:
+                ty, tz = step(yy, others[k][0]), step(zz, others[k][1])
+                win = window(ty * SIDE + tz)
+                a2.append(send(src.at[:, win], dst.at[yy, zz], a2_send.at[n, k], a2_recv.at[n, k], dev(ty, tz)))
     mine = window(chip)
     own = [
         pltpu.make_async_copy(gate.at[:, mine], gp.at[yy, zz], loc.at[6]),
@@ -210,23 +219,21 @@
     ]
     for copy in own:
         copy.start()
-    for half in (0, 1):
-        pass_on(half, 1)
-        pass_on(half, 2)
-    lax.fori_loop(48, 96, one_slot, 0)
-    for half in (0, 1):
-        pass_on(half, 3)
+    hid = []
+
+    def send_hidden(some):
+        for k in some:
+            ty, tz = step(yy, others[k][0]), step(zz, others[k][1])
+            hid.append(send(hs.at[ty * SIDE + tz], hr.at[chip], h_send.at[k], h_recv.at[k], dev(ty, tz)))
+
+    send_hidden(range(len(others)))
+    own_h = pltpu.make_async_copy(hs.at[chip], hr.at[chip], loc.at[8])
+    own_h.start()
+
     for j in range(4):
         for half in (0, 1):
             got[half, 6 + 4 * j].wait_recv()
             got[half, 7 + 4 * j].wait_recv()
-
-    hid = []
-    for k, (dy, dz) in enumerate(others):
-        ty, tz = step(yy, dy), step(zz, dz)
-        hid.append(send(hs.at[ty * SIDE + tz], hr.at[chip], h_send.at[k], h_recv.at[k], dev(ty, tz)))
-    own_h = pltpu.make_async_copy(hs.at[chip], hr.at[chip], loc.at[8])
-    own_h.start()
 
     local[0].wait()
 
@@ -249,13 +256,7 @@
 
     lax.fori_loop(0, 6, dh_tile, 0)
 
-    for copy in own:
-        copy.wait()
-    for copy in a2:
-        copy.wait_recv()
-
-    def point(i, carry):
-        a, b = lax.div(i, SIDE), lax.rem(i, SIDE)
+    def point(a, b):
         for k in range(WIN // 128):
             lane = pl.ds(k * 128, 128)
             activated, slope = gelu_pair(gp[a, b, :, lane].astype(F32))
@@ -263,9 +264,26 @@
             u = uq[a, b, :, lane].astype(F32)
             lg[a, b, :, lane] = (dh * u * slope).astype(BF)
             gp[a, b, :, lane] = (dh * activated).astype(BF)
-        return carry
-
-    lax.fori_loop(0, SIDE * SIDE, point, 0)
+
+    def near_of(i):
+        return i + lax.div(i, 2)
+
+    def point_y(i, carry):
+        point(step(yy, 2), i)
+        return carry
+
+    def point_z(i, carry):
+        point(step(yy, near_of(i)), step(zz, 2))
+        return carry
+
+    def point_near(i, carry):
+        point(step(yy, near_of(lax.div(i, 3))), step(zz, near_of(lax.rem(i, 3))))
+        return carry
+
+    for copy in a2[: 2 * n_far]:
+        copy.wait_recv()
+    lax.fori_loop(0, SIDE, point_y, 0)
+    lax.fori_loop(0, SIDE - 1, point_z, 0)
     for n in (2, 3):
         local[n].wait()
     for n in (1, 2):
@@ -383,6 +401,12 @@
                 r1[half, c, k].wait_recv()
             add_rows(half, c, p, 0, (3, 4))
             add_rows(half, c, p, 1, (2, 5))
+            if c == LAST:
+                for part in (0, 1):
+                    rs2(half, c, part, step(q, 2), part, 2)
+                    rs2(half, c, 2 + part, step(q, 1), part, 1)
+                    rs2(half, c, 4 + part, step(q, -1), part, -1)
+                continue
             rs2(half, c, 0, step(q, 2), 0, 1)
             rs2(half, c, 1, step(q, 2), 1, -1)
             rs2(half, c, 2, step(q, 1), 1, 1)
@@ -404,9 +428,9 @@
         first, width = CHUNKS[c]
         for half in (0, 1):
             p, q = pos[half]
-            for k in (2, 3, 4, 5):
+            for k in range(6) if c == LAST else (2, 3, 4, 5):
                 r2[half, c, k].wait_recv()
-            for part, bufs in ((0, (3, 4)), (1, (2, 5))):
+            for part, bufs in ((0, (0, 2, 4)), (1, (1, 3, 5))) if c == LAST else ((0, (3, 4)), (1, (2, 5))):
                 total = t[piece_t(half, c, q, part)].astype(F32)
                 for k in bufs:
                     total = total + rc[half, k, :, held(c)].astype(F32)
@@ -418,15 +442,25 @@
             ))
 
     far(0)
+    far(1)
+    for copy in own:
+        copy.wait()
+    for copy in a2[2 * n_far :]:
+        copy.wait_recv()
+    lax.fori_loop(0, (SIDE - 1) * (SIDE - 1), point_near, 0)
     near_terms(0)
-    far(1)
     relay(0)
+    near_terms(1)
     own_terms(0)
-    near_terms(1)
+    relay(1)
     own_terms(1)
     turn(0)
-    relay(1)
+    own_terms(2)
+    far(2)
     relay2(0)
+    turn(1)
+    near_terms(2)
+    relay(2)
 
     own_h.wait()
     for copy in hid:
@@ -439,9 +473,10 @@
     p_copy = send(pb.at[pl.ds((1 - core) * CAP, CAP)], pr, p_send.at[0], p_recv.at[0], partner)
 
     finish(0)
-    turn(1)
     relay2(1)
+    turn(2)
     finish(1)
+    finish(2)
     p_copy.wait_recv()
     for k in range(CAP):
         present = slots[2, me * CAP + k].astype(F32)
@@ -491,9 +526,9 @@
             dma((2, 20)), dma((2, 20)),
             dma((2, 15)), dma((2, 15)),
             dma((15,)), dma((15,)),
-            dma((2, 12)), dma((2, 12)),
-            dma((2, 12)), dma((2, 12)),
-            dma((2, 2)), dma((2, 2)),
+            dma((2, 18)), dma((2, 18)),
+            dma((2, 18)), dma((2, 18)),
+            dma((2, 3)), dma((2, 3)),
             dma((1,)), dma((1,)),
         ],
         compiler_params=pltpu.CompilerParams(

time: 130 us -> 125 us (0.962)
  Pallas kernels: 126 us -> 121 us
    pallas_call x1, Pallas kernels: 126 us -> 121 us  [shards(): pl.pallas_call(kernel, out_shape=(jax.ShapeDtypeStruct((TOK, WIDTH), BF),...]
where the time goes in v4:
time: 125 us
  Pallas kernels  121 us (97%)
  local copies, waits for them, and re-layouts  3.31 us (3%)
    pallas_call x1, Pallas kernels, shards(): pl.pallas_call(kernel, out_shape=(jax.ShapeDtypeStruct((TOK, WIDTH), BF),...  121 us
    unnamed x2, local copies, waits for them, and re-layouts  3.31 us

profile of v4, /device:TPU:0, one launch (start us, length us, event | category | flops | bytes accessed | tf_op | source)
XLA Modules:
  0.0 125.0 jit_solution(8284560983354331680)
XLA Ops:
  0.6 121.1 %relay.1 = (bf16[48,4096]{1,0:T(8,128)(2,1)}, bf16[3,128,128]{2,1,0:T(8,128)(2,1)}) custom-call(s32[1,64]{1,0:T(1,128)} %block_rows.1, s32[1,64]{1,0:T(1,128)} %block_cols.1, s32[1,64]{1,0:T(1,128)} %block_owner.1, bf16[48,4096]{1,0:T(8,128)(2,1)} %bitcast.13, bf16[352,4096]{1,0:T(8,128)(2,1)} %bitcast.8, bf16[352,4096]{1,0:T(8,128)(2,1)} %bitcast.9, ...), custom_call_target="tpu_custom_call" | custom-call | tf_op jit(solution)/shard_map/relay/pallas_call | solution.py:495
  121.7 1.8 %copy.13 = bf16[1,48,4096]{2,1,0:T(8,128)(2,1)} copy(bf16[1,48,4096]{2,1,0:T(8,128)(2,1)} %bitcast.14) | data formatting | bytes 786432
  123.5 1.5 %copy.14 = bf16[1,3,128,128]{3,2,1,0:T(8,128)(2,1)} copy(bf16[1,3,128,128]{3,2,1,0:T(8,128)(2,1)} %bitcast.15) | data formatting | bytes 196608

commit v5 on v4

--- a/solution.py
+++ b/solution.py
@@ -34,7 +34,7 @@
 def kernel(
     block_rows, block_cols, block_owner, d_out, w_down, w_gate, w_up, gate, up,
     grad_out, block_out,
-    wd, wg, wu, x, gp, uq, lg, t, rb, rc, fin, gl, ul, xb, hs, hr, pb, pr, tab, slots,
+    wd, wg, wu, x, gp, uq, lg, t, rb, rc, fin, gl, ul, xb, hs, hr, pb, pr, tab, slots, done,
     loc, w_send, w_recv, ag_send, ag_recv, a2_send, a2_recv, h_send, h_recv,
     rb_send, rb_recv, rc_send, rc_recv, x_send, x_recv, p_send, p_recv,
 ):
@@ -163,34 +163,6 @@
     for half in (0, 1):
         pass_on(half, 0)
 
-    blocks = block_owner.shape[1]
-    row_id = lax.broadcasted_iota(jnp.int32, (blocks, blocks), 0)
-    col_id = lax.broadcasted_iota(jnp.int32, (blocks, blocks), 1)
-
-    def upright(ref):
-        wide = jnp.broadcast_to(ref[...], (blocks, blocks))
-        return jnp.sum(jnp.where(row_id == col_id, wide, 0), axis=1, keepdims=True)
-
-    owner = upright(block_owner)
-    earlier = (block_owner[...] == owner) & (col_id < row_id)
-    position = owner * CAP + jnp.sum(jnp.where(earlier, 1, 0), axis=1, keepdims=True)
-    match = position == lax.broadcasted_iota(jnp.int32, (blocks, 128), 1)
-    for k, value in enumerate((upright(block_rows), upright(block_cols), jnp.ones((blocks, 1), jnp.int32))):
-        tab[k : k + 1, :] = jnp.sum(jnp.where(match, value, 0), axis=0, keepdims=True)
-    tables = pltpu.make_async_copy(tab, slots, loc.at[10])
-    tables.start()
-    tables.wait()
-
-    pltpu.make_async_copy(gl, gl, loc.at[1]).wait()
-    pltpu.make_async_copy(ul, ul, loc.at[2]).wait()
-
-    def one_slot(s, carry):
-        g = gl[slots[0, s]].astype(F32)
-        u = ul[slots[0, s]].astype(F32)
-        hs[lax.div(s, 6), lax.rem(s, 6)] = (gelu_pair(g)[0] * u).astype(BF)
-        return carry
-
-    lax.fori_loop(0, 48, one_slot, 0)
     for half in (0, 1):
         got[half, 2].wait_recv()
         got[half, 3].wait_recv()
@@ -199,7 +171,6 @@
     for half in (0, 1):
         pass_on(half, 1)
         pass_on(half, 2)
-    lax.fori_loop(48, 96, one_slot, 0)
     for half in (0, 1):
         pass_on(half, 3)
     def window(g):
@@ -219,6 +190,34 @@
     ]
     for copy in own:
         copy.start()
+    blocks = block_owner.shape[1]
+    row_id = lax.broadcasted_iota(jnp.int32, (blocks, blocks), 0)
+    col_id = lax.broadcasted_iota(jnp.int32, (blocks, blocks), 1)
+
+    def upright(ref):
+        wide = jnp.broadcast_to(ref[...], (blocks, blocks))
+        return jnp.sum(jnp.where(row_id == col_id, wide, 0), axis=1, keepdims=True)
+
+    owner = upright(block_owner)
+    earlier = (block_owner[...] == owner) & (col_id < row_id)
+    position = owner * CAP + jnp.sum(jnp.where(earlier, 1, 0), axis=1, keepdims=True)
+    match = position == lax.broadcasted_iota(jnp.int32, (blocks, 128), 1)
+    for k, value in enumerate((upright(block_rows), upright(block_cols), jnp.ones((blocks, 1), jnp.int32))):
+        tab[k : k + 1, :] = jnp.sum(jnp.where(match, value, 0), axis=0, keepdims=True)
+    tables = pltpu.make_async_copy(tab, slots, loc.at[10])
+    tables.start()
+    tables.wait()
+
+    pltpu.make_async_copy(gl, gl, loc.at[1]).wait()
+    pltpu.make_async_copy(ul, ul, loc.at[2]).wait()
+
+    def one_slot(s, carry):
+        g = gl[slots[0, s]].astype(F32)
+        u = ul[slots[0, s]].astype(F32)
+        hs[lax.div(s, 6), lax.rem(s, 6)] = (gelu_pair(g)[0] * u).astype(BF)
+        return carry
+
+    lax.fori_loop(0, 96, one_slot, 0)
     hid = []
 
     def send_hidden(some):
@@ -476,11 +475,14 @@
     relay2(1)
     turn(2)
     finish(1)
-    finish(2)
     p_copy.wait_recv()
     for k in range(CAP):
         present = slots[2, me * CAP + k].astype(F32)
-        block_out[k] = ((pb[core * CAP + k] + pr[k]) * ((1.0 / 32.0) * present)).astype(BF)
+        done[k] = ((pb[core * CAP + k] + pr[k]) * ((1.0 / 32.0) * present)).astype(BF)
+    done_copy = pltpu.make_async_copy(done, block_out, loc.at[11])
+    done_copy.start()
+    finish(2)
+    done_copy.wait()
     for copy in last:
         copy.wait_recv()
     for copy in started:
@@ -499,7 +501,7 @@
             jax.ShapeDtypeStruct((CAP, 128, 128), BF),
         ),
         in_specs=[vmem] * 3 + [hbm] * 6,
-        out_specs=(hbm, vmem),
+        out_specs=(hbm, hbm),
         scratch_shapes=[
             pltpu.VMEM((WIN, WIDTH), BF),
             pltpu.VMEM((WIN, WIDTH), BF),
@@ -521,7 +523,8 @@
             pltpu.VMEM((CAP, 128, 128), F32),
             pltpu.VMEM((8, 128), jnp.int32),
             pltpu.SMEM((8, 128), jnp.int32),
-            dma((11,)),
+            pltpu.VMEM((CAP, 128, 128), BF),
+            dma((12,)),
             dma((3,)), dma((3,)),
             dma((2, 20)), dma((2, 20)),
             dma((2, 15)), dma((2, 15)),

time: 125 us -> 125 us (level)
  no operation moved by 1% of the time
where the time goes in v5:
time: 125 us; the launch traced here: 124 us
  Pallas kernels  120 us (96%)
  local copies, waits for them, and re-layouts  3.31 us (3%)
    pallas_call x1, Pallas kernels, shards(): pl.pallas_call(kernel, out_shape=(jax.ShapeDtypeStruct((TOK, WIDTH), BF),...  120 us
    unnamed x2, local copies, waits for them, and re-layouts  3.31 us

profile of v5, /device:TPU:0, one launch (start us, length us, event | category | flops | bytes accessed | tf_op | source)
XLA Modules:
  0.0 124.4 jit_solution(13489358153530922408)
XLA Ops:
  0.6 120.5 %relay.1 = (bf16[48,4096]{1,0:T(8,128)(2,1)}, bf16[3,128,128]{2,1,0:T(8,128)(2,1)}) custom-call(s32[1,64]{1,0:T(1,128)} %block_rows.1, s32[1,64]{1,0:T(1,128)} %block_cols.1, s32[1,64]{1,0:T(1,128)} %block_owner.1, bf16[48,4096]{1,0:T(8,128)(2,1)} %bitcast.13, bf16[352,4096]{1,0:T(8,128)(2,1)} %bitcast.8, bf16[352,4096]{1,0:T(8,128)(2,1)} %bitcast.9, ...), custom_call_target="tpu_custom_call" | custom-call | tf_op jit(solution)/shard_map/relay/pallas_call | solution.py:497
  121.1 1.8 %copy.13 = bf16[1,48,4096]{2,1,0:T(8,128)(2,1)} copy(bf16[1,48,4096]{2,1,0:T(8,128)(2,1)} %bitcast.14) | data formatting | bytes 786432
  122.9 1.5 %copy.14 = bf16[1,3,128,128]{3,2,1,0:T(8,128)(2,1)} copy(bf16[1,3,128,128]{3,2,1,0:T(8,128)(2,1)} %bitcast.15) | data formatting | bytes 196608

commit v6 on v5

--- a/solution.py
+++ b/solution.py
@@ -16,7 +16,7 @@
 WIN = 768
 HALF = WIDTH // 2
 QUART = WIDTH // 4
-CHUNKS = ((0, 1024), (1024, 768), (1792, 256))
+CHUNKS = ((0, 1280), (1280, 512), (1792, 256))
 LAST = len(CHUNKS) - 1
 
 

time: 125 us -> 125 us (level)
  no operation moved by 1% of the time
where the time goes in v6:
time: 125 us
  Pallas kernels  121 us (97%)
  local copies, waits for them, and re-layouts  3.31 us (3%)
    pallas_call x1, Pallas kernels, shards(): pl.pallas_call(kernel, out_shape=(jax.ShapeDtypeStruct((TOK, WIDTH), BF),...  121 us
    unnamed x2, local copies, waits for them, and re-layouts  3.31 us

profile of v6, /device:TPU:0, one launch (start us, length us, event | category | flops | bytes accessed | tf_op | source)
XLA Modules:
  0.0 124.5 jit_solution(16629791286471337336)
XLA Ops:
  0.6 120.6 %relay.1 = (bf16[48,4096]{1,0:T(8,128)(2,1)}, bf16[3,128,128]{2,1,0:T(8,128)(2,1)}) custom-call(s32[1,64]{1,0:T(1,128)} %block_rows.1, s32[1,64]{1,0:T(1,128)} %block_cols.1, s32[1,64]{1,0:T(1,128)} %block_owner.1, bf16[48,4096]{1,0:T(8,128)(2,1)} %bitcast.13, bf16[352,4096]{1,0:T(8,128)(2,1)} %bitcast.8, bf16[352,4096]{1,0:T(8,128)(2,1)} %bitcast.9, ...), custom_call_target="tpu_custom_call" | custom-call | tf_op jit(solution)/shard_map/relay/pallas_call | solution.py:497
  121.2 1.8 %copy.13 = bf16[1,48,4096]{2,1,0:T(8,128)(2,1)} copy(bf16[1,48,4096]{2,1,0:T(8,128)(2,1)} %bitcast.14) | data formatting | bytes 786432
  123.0 1.5 %copy.14 = bf16[1,3,128,128]{3,2,1,0:T(8,128)(2,1)} copy(bf16[1,3,128,128]{3,2,1,0:T(8,128)(2,1)} %bitcast.15) | data formatting | bytes 196608
